TPU v7x, 32 devices: a whole 2x2x4 slice. The times are simulated.
32 devices in a mesh: dp: 8 (over z, x), seq: 4 (over y, core).
Axes of the slice: x: 2, y: 2, z: 4, core: 2. Of those that a mesh axis runs over, the one named last changes fastest.
Arguments:
- tokens: bfloat16 [16384, 1024], P(('dp', 'seq')), may hold values from -6 to 6
- time_embed: bfloat16 [32, 1024], P(('dp', 'seq')), may hold values from -6 to 6
- lengths: int32 [32], P('dp'), may hold values from 0 to 475, as said below
- cotangent: bfloat16 [16384, 1024], P(('dp', 'seq')), may hold values from -6 to 6
- w_query: bfloat16 [1024, 1024], P('seq'), may hold values from -0.1875 to 0.1875
- w_key: bfloat16 [1024, 1024], P('seq'), may hold values from -0.1875 to 0.1875
- w_value: bfloat16 [1024, 1024], P('seq'), may hold values from -0.1875 to 0.1875
- w_out: bfloat16 [1024, 1024], P('seq'), may hold values from -0.75 to 0.75
- w_time: bfloat16 [1024, 1024], P('seq'), may hold values from -0.1875 to 0.1875
- w_in: bfloat16 [4096, 1024], P('seq'), may hold values from -0.1875 to 0.1875
- w_down: bfloat16 [4096, 1024], P('seq'), may hold values from -0.09375 to 0.09375
- b_query: bfloat16 [1024], replicated, may hold values from -3 to 3
- b_value: bfloat16 [1024], replicated, may hold values from -3 to 3
- b_out: bfloat16 [1024], replicated, may hold values from -3 to 3
- b_time: bfloat16 [1024], replicated, may hold values from -3 to 3
- b_in: bfloat16 [4096], replicated, may hold values from -3 to 3
- b_down: bfloat16 [1024], replicated, may hold values from -2 to 2
- gain_one: bfloat16 [1024], replicated, may hold values from 0.25 to 1.75
- shift_one: bfloat16 [1024], replicated, may hold values from -2 to 2
- gain_two: bfloat16 [1024], replicated, may hold values from 0.25 to 1.75
- shift_two: bfloat16 [1024], replicated, may hold values from -2 to 2
Outputs:
- layer_out: bfloat16 [16384, 1024], P(('dp', 'seq'))
- grad_tokens: bfloat16 [16384, 1024], P(('dp', 'seq'))
- grad_w_query: float32 [1024, 1024], P('seq')
- grad_w_key: float32 [1024, 1024], P('seq')
- grad_w_value: float32 [1024, 1024], P('seq')
- grad_w_out: float32 [1024, 1024], P('seq')
- grad_w_time: float32 [1024, 1024], P('seq')
- grad_w_in: float32 [4096, 1024], P('seq')
- grad_w_down: float32 [4096, 1024], P('seq')
- grad_b_query: float32 [1024], replicated
- grad_b_value: float32 [1024], replicated
- grad_b_out: float32 [1024], replicated
- grad_b_time: float32 [1024], replicated
- grad_b_in: float32 [4096], replicated
- grad_b_down: float32 [1024], replicated
- grad_gain_one: float32 [1024], replicated
- grad_shift_one: float32 [1024], replicated
- grad_gain_two: float32 [1024], replicated
- grad_shift_two: float32 [1024], replicated
Inputs may be any that keep to these rules, and one draw needn't show every extreme that they name: Item i's valid slots are its first lengths[i] + 25; every draw has an item of length 475 and one of length 0.
All inputs are finite; a program needn't handle non-finite values.
Results may differ from a plain program's by a relative error of at most 0.02.
Values may be sent and summed in bfloat16 or wider, within the bound.
A program may use at most 256 MiB of HBM per device.

v0:
```python
import jax
import jax.numpy as jnp
from jax import lax
from jax.sharding import PartitionSpec as P

HEAD_DIM = 64
BLOCK = 25


norm_eps = 1e-05
neg_large = -1e30


def layer_norm(values, gain, shift):
    center = values - jnp.mean(values, axis=-1, keepdims=True)
    spread = lax.rsqrt(jnp.mean(center * center, axis=-1, keepdims=True) + norm_eps)
    return center * spread * gain + shift


def exact_gelu(values):
    return jax.nn.gelu(values, approximate=False)


def split_heads(rows):
    return rows.reshape(rows.shape[0], rows.shape[1] // HEAD_DIM, HEAD_DIM)


def item_scores(item_block, key_valid):
    queries = split_heads(item_block[:, 0])
    key_heads = split_heads(item_block[:, 1])
    value_heads = split_heads(item_block[:, 2])
    scores = jnp.einsum(
        "qhd,khd->hqk", queries, key_heads, preferred_element_type=jnp.float32
    ) * HEAD_DIM ** (-0.5)
    masked = jnp.where(key_valid[None, None, :], scores, neg_large)
    return (queries, key_heads, value_heads, masked)


def attend_forward(packed):
    item_block, key_valid = packed
    queries, key_heads, value_heads, masked = item_scores(item_block, key_valid)
    row_max = jnp.max(masked, axis=-1, keepdims=True)
    exp_scores = jnp.exp(masked - row_max)
    row_total = jnp.sum(exp_scores, axis=-1, keepdims=True)
    soft_weights = (exp_scores / row_total).astype(jnp.bfloat16)
    mixed_heads = jnp.einsum(
        "hqk,khd->qhd", soft_weights, value_heads, preferred_element_type=jnp.float32
    )
    log_total = row_max[:, :, 0] + jnp.log(row_total[:, :, 0])
    return (mixed_heads.reshape(item_block.shape[0], -1).astype(jnp.bfloat16), log_total)


def attend_backward(packed):
    item_block, key_valid, log_total, grad_block = packed
    queries, key_heads, value_heads, masked = item_scores(item_block, key_valid)
    soft_weights = jnp.exp(masked - log_total[:, :, None])
    grad_heads = split_heads(grad_block)
    grad_value = jnp.einsum(
        "hqk,qhd->khd",
        soft_weights.astype(jnp.bfloat16),
        grad_heads,
        preferred_element_type=jnp.float32,
    )
    grad_soft = jnp.einsum(
        "qhd,khd->hqk", grad_heads, value_heads, preferred_element_type=jnp.float32
    )
    grad_scores = soft_weights * (
        grad_soft - jnp.sum(soft_weights * grad_soft, axis=-1, keepdims=True)
    )
    scores_low = grad_scores.astype(jnp.bfloat16)
    score_scale = HEAD_DIM ** (-0.5)
    grad_query = (
        jnp.einsum("hqk,khd->qhd", scores_low, key_heads, preferred_element_type=jnp.float32)
        * score_scale
    )
    grad_key = (
        jnp.einsum("hqk,qhd->khd", scores_low, queries, preferred_element_type=jnp.float32)
        * score_scale
    )
    slot_count = item_block.shape[0]
    return jnp.stack(
        [
            grad_query.reshape(slot_count, -1),
            grad_key.reshape(slot_count, -1),
            grad_value.reshape(slot_count, -1),
        ],
        axis=1,
    ).astype(jnp.bfloat16)


def local(
    tokens,
    time_embed,
    lengths,
    cotangent,
    w_query,
    w_key,
    w_value,
    w_out,
    w_time,
    w_in,
    w_down,
    b_query,
    b_value,
    b_out,
    b_time,
    b_in,
    b_down,
    gain_one,
    shift_one,
    gain_two,
    shift_two,
):
    seq_rank = lax.axis_index("seq")
    item_count = time_embed.shape[0]
    token_count = tokens.shape[0]
    slot_count = token_count // item_count
    model_width = tokens.shape[1]
    full_query, full_key, full_value, full_out, full_time, full_in, full_down = (
        lax.all_gather(w_query, "seq", axis=0, tiled=True),
        lax.all_gather(w_key, "seq", axis=0, tiled=True),
        lax.all_gather(w_value, "seq", axis=0, tiled=True),
        lax.all_gather(w_out, "seq", axis=0, tiled=True),
        lax.all_gather(w_time, "seq", axis=0, tiled=True),
        lax.all_gather(w_in, "seq", axis=0, tiled=True),
        lax.all_gather(w_down, "seq", axis=0, tiled=True),
    )
    bias_query = b_query.astype(jnp.float32)
    bias_value = b_value.astype(jnp.float32)
    bias_out = b_out.astype(jnp.float32)
    bias_time = b_time.astype(jnp.float32)
    bias_in = b_in.astype(jnp.float32)
    bias_down = b_down.astype(jnp.float32)
    gain_first = gain_one.astype(jnp.float32)
    shift_first = shift_one.astype(jnp.float32)
    gain_last = gain_two.astype(jnp.float32)
    shift_last = shift_two.astype(jnp.float32)
    slot_index = lax.broadcasted_iota(jnp.int32, (lengths.shape[0], slot_count), 1)
    group_valid = slot_index < lengths[:, None] + BLOCK
    own_valid = lax.dynamic_slice_in_dim(group_valid, seq_rank * item_count, item_count, 0)
    row_keep = own_valid.reshape(token_count, 1).astype(jnp.float32)
    time_proj = jnp.dot(time_embed, full_time, preferred_element_type=jnp.float32) + bias_time
    resid = (tokens.reshape(item_count, slot_count, model_width) + time_proj[:, None, :]).reshape(
        token_count, model_width
    )
    resid_low = resid.astype(jnp.bfloat16)
    query_rows = (
        jnp.dot(resid_low, full_query, preferred_element_type=jnp.float32) + bias_query
    ).astype(jnp.bfloat16)
    key_rows = jnp.dot(resid_low, full_key, preferred_element_type=jnp.float32).astype(jnp.bfloat16)
    value_rows = (
        jnp.dot(resid_low, full_value, preferred_element_type=jnp.float32) + bias_value
    ).astype(jnp.bfloat16)
    stacked = jnp.stack([query_rows, key_rows, value_rows], axis=1).reshape(
        item_count, slot_count, 3, model_width
    )
    head_side = lax.all_to_all(stacked, "seq", split_axis=3, concat_axis=0, tiled=True)
    mixed_heads, log_totals = lax.map(attend_forward, (head_side, group_valid))
    mixed_rows = lax.all_to_all(
        mixed_heads, "seq", split_axis=0, concat_axis=2, tiled=True
    ).reshape(token_count, model_width)
    attn_out = jnp.dot(mixed_rows, full_out, preferred_element_type=jnp.float32) + bias_out
    first_norm, first_pull = jax.vjp(layer_norm, resid + attn_out, gain_first, shift_first)
    first_low = first_norm.astype(jnp.bfloat16)
    hidden_pre = (
        jnp.einsum("td,fd->tf", first_low, full_in, preferred_element_type=jnp.float32) + bias_in
    )
    hidden, gelu_pull = jax.vjp(exact_gelu, hidden_pre)
    hidden_low = hidden.astype(jnp.bfloat16)
    ffn_out = jnp.dot(hidden_low, full_down, preferred_element_type=jnp.float32) + bias_down
    second_norm, second_pull = jax.vjp(layer_norm, first_norm + ffn_out, gain_last, shift_last)
    layer_out = (second_norm * row_keep).astype(jnp.bfloat16)
    back_query, back_key, back_value, back_out, back_in, back_down = (
        lax.all_gather(w_query, "seq", axis=0, tiled=True),
        lax.all_gather(w_key, "seq", axis=0, tiled=True),
        lax.all_gather(w_value, "seq", axis=0, tiled=True),
        lax.all_gather(w_out, "seq", axis=0, tiled=True),
        lax.all_gather(w_in, "seq", axis=0, tiled=True),
        lax.all_gather(w_down, "seq", axis=0, tiled=True),
    )
    grad_second_in, grad_gain_two, grad_shift_two = second_pull(
        cotangent.astype(jnp.float32) * row_keep
    )
    grad_ffn = grad_second_in.astype(jnp.bfloat16)
    grad_hidden = jnp.einsum("td,fd->tf", grad_ffn, back_down, preferred_element_type=jnp.float32)
    grad_pre = gelu_pull(grad_hidden)[0].astype(jnp.bfloat16)
    grad_first = grad_second_in + jnp.dot(grad_pre, back_in, preferred_element_type=jnp.float32)
    grad_first_in, grad_gain_one, grad_shift_one = first_pull(grad_first)
    grad_attn = grad_first_in.astype(jnp.bfloat16)
    grad_mixed = jnp.einsum(
        "td,ed->te", grad_attn, back_out, preferred_element_type=jnp.float32
    ).astype(jnp.bfloat16)
    grad_heads = lax.all_to_all(
        grad_mixed.reshape(item_count, slot_count, model_width),
        "seq",
        split_axis=2,
        concat_axis=0,
        tiled=True,
    )
    grad_stack = lax.map(attend_backward, (head_side, group_valid, log_totals, grad_heads))
    grad_qkv = lax.all_to_all(grad_stack, "seq", split_axis=0, concat_axis=3, tiled=True).reshape(
        token_count, 3, model_width
    )
    grad_query_rows = grad_qkv[:, 0]
    grad_key_rows = grad_qkv[:, 1]
    grad_value_rows = grad_qkv[:, 2]
    grad_resid = grad_first_in + jnp.einsum(
        "te,de->td", grad_query_rows, back_query, preferred_element_type=jnp.float32
    )
    grad_resid = grad_resid + jnp.einsum(
        "te,de->td", grad_key_rows, back_key, preferred_element_type=jnp.float32
    )
    grad_resid = grad_resid + jnp.einsum(
        "te,de->td", grad_value_rows, back_value, preferred_element_type=jnp.float32
    )
    grad_tokens = grad_resid.astype(jnp.bfloat16)
    grad_time = jnp.sum(grad_resid.reshape(item_count, slot_count, model_width), axis=1).astype(
        jnp.bfloat16
    )
    term_in = jnp.einsum("tf,td->fd", grad_pre, first_low, preferred_element_type=jnp.float32)
    term_down = jnp.einsum("tf,td->fd", hidden_low, grad_ffn, preferred_element_type=jnp.float32)
    ffn_share = lax.psum_scatter(
        jnp.concatenate([term_in, term_down], axis=1).astype(jnp.bfloat16),
        "seq",
        scatter_dimension=0,
        tiled=True,
    ).astype(jnp.float32)
    share_in = ffn_share[:, :model_width]
    share_down = ffn_share[:, model_width:]
    grad_qkv_flat = grad_qkv.reshape(token_count, 3 * model_width)
    term_qkv = jnp.einsum("tr,te->re", resid_low, grad_qkv_flat, preferred_element_type=jnp.float32)
    term_out = jnp.einsum("tr,te->re", mixed_rows, grad_attn, preferred_element_type=jnp.float32)
    term_time = jnp.einsum("tr,te->re", time_embed, grad_time, preferred_element_type=jnp.float32)
    attn_share = lax.psum_scatter(
        jnp.concatenate([term_qkv, term_out, term_time], axis=1).astype(jnp.bfloat16),
        "seq",
        scatter_dimension=0,
        tiled=True,
    ).astype(jnp.float32)
    sum_in, sum_down, sum_attn = lax.psum((share_in, share_down, attn_share), "dp")
    (
        grad_b_query,
        grad_b_value,
        grad_b_out,
        grad_b_time,
        grad_b_in,
        grad_b_down,
        sum_gain_one,
        sum_shift_one,
        sum_gain_two,
        sum_shift_two,
    ) = lax.psum(
        (
            jnp.sum(grad_query_rows, axis=0, dtype=jnp.float32),
            jnp.sum(grad_value_rows, axis=0, dtype=jnp.float32),
            jnp.sum(grad_attn, axis=0, dtype=jnp.float32),
            jnp.sum(grad_time, axis=0, dtype=jnp.float32),
            jnp.sum(grad_pre, axis=0, dtype=jnp.float32),
            jnp.sum(grad_ffn, axis=0, dtype=jnp.float32),
            grad_gain_one,
            grad_shift_one,
            grad_gain_two,
            grad_shift_two,
        ),
        ("dp", "seq"),
    )
    return (
        layer_out,
        grad_tokens,
        sum_attn[:, :model_width],
        sum_attn[:, model_width : 2 * model_width],
        sum_attn[:, 2 * model_width : 3 * model_width],
        sum_attn[:, 3 * model_width : 4 * model_width],
        sum_attn[:, 4 * model_width :],
        sum_in,
        sum_down,
        grad_b_query,
        grad_b_value,
        grad_b_out,
        grad_b_time,
        grad_b_in,
        grad_b_down,
        sum_gain_one,
        sum_shift_one,
        sum_gain_two,
        sum_shift_two,
    )


def solution(mesh):
    in_specs = (
        P(("dp", "seq"), None),
        P(("dp", "seq"), None),
        P("dp"),
        P(("dp", "seq"), None),
        P("seq", None),
        P("seq", None),
        P("seq", None),
        P("seq", None),
        P("seq", None),
        P("seq", None),
        P("seq", None),
        P(),
        P(),
        P(),
        P(),
        P(),
        P(),
        P(),
        P(),
        P(),
        P(),
    )
    out_specs = (
        P(("dp", "seq"), None),
        P(("dp", "seq"), None),
        P("seq", None),
        P("seq", None),
        P("seq", None),
        P("seq", None),
        P("seq", None),
        P("seq", None),
        P("seq", None),
        P(),
        P(),
        P(),
        P(),
        P(),
        P(),
        P(),
        P(),
        P(),
        P(),
    )
    return jax.shard_map(local, mesh=mesh, in_specs=in_specs, out_specs=out_specs, check_vma=False)
```

profile of v0, /device:TPU:0, one launch (start us, length us, event | category | flops | bytes accessed | tf_op | source)
XLA Modules:
  0.0 1024.9 jit_solution(11175937221474394372)
XLA Ops:
  11.2 23.7 %all-gather.8.cloned.1.call-done = bf16[1024,1024]{1,0:T(8,128)(2,1)} async-done(((bf16[256,1024]{1,0:T(8,128)(2,1)}), bf16[1024,1024]{1,0:T(8,128)(2,1)}) %all-gather.8.cloned.1.call-update) | async-done | bytes 2097168 | tf_op jit(solution)/shard_map/all_gather | solution.py:124
  34.9 2.0 fusion.40
  36.9 22.2 %all-gather.12.cloned.1.call-done = bf16[1024,1024]{1,0:T(8,128)(2,1)} async-done(((bf16[256,1024]{1,0:T(8,128)(2,1)}), bf16[1024,1024]{1,0:T(8,128)(2,1)}) %all-gather.12.cloned.1.call-update) | async-done | bytes 2097168 | tf_op jit(solution)/shard_map/all_gather | solution.py:121
  59.1 3.8 fusion.28
  62.9 20.3 %all-gather.10.cloned.1.call-done = bf16[1024,1024]{1,0:T(8,128)(2,1)} async-done(((bf16[256,1024]{1,0:T(8,128)(2,1)}), bf16[1024,1024]{1,0:T(8,128)(2,1)}) %all-gather.10.cloned.1.call-update) | async-done | bytes 2097168 | tf_op jit(solution)/shard_map/all_gather | solution.py:120
  83.2 3.8 fusion.30
  87.1 20.2 %all-gather.14.cloned.1.call-done = bf16[1024,1024]{1,0:T(8,128)(2,1)} async-done(((bf16[256,1024]{1,0:T(8,128)(2,1)}), bf16[1024,1024]{1,0:T(8,128)(2,1)}) %all-gather.14.cloned.1.call-update) | async-done | bytes 2097168 | tf_op jit(solution)/shard_map/all_gather | solution.py:122
  107.3 3.0 fusion.31
  110.6 5.7 copy.80
  116.3 5.1 all-to-all-start
  122.3 77.5 %all-to-all-done = bf16[1,512,3,1024]{1,2,0,3:T(4,128)(2,1)} async-done(((bf16[1,512,3,1024]{1,2,0,3:T(4,128)(2,1)}), bf16[1,512,3,1024]{1,2,0,3:T(4,128)(2,1)}, u32[]{:S(2)}, u32[]{:S(2)}) %all-to-all-start) | async-done | bytes 3145760 | tf_op jit(solution)/shard_map/all_to_all | solution.py:157
  199.8 3.0 copy.97
  202.9 16.3 %while.22 = (s32[]{:T(128)}, bf16[4,512,256]{1,2,0:T(8,128)(2,1)}, f32[4,4,512]{2,1,0:T(4,128)S(1)}, bf16[4,512,3,256]{1,3,2,0:T(8,128)(2,1)S(1)}, pred[4,512]{1,0:T(4,128)(4,1)S(1)}, /*index=5*/s32[]{:T(128)}) while((s32[]{:T(128)}, bf16[4,512,256]{1,2,0:T(8,128)(2,1)}, f32[4,4,512]{2,1,0:T(4,128)S(1)}, ...), condition=%wide.region_3.4_spmd, body=%wide.region_0.3_spmd.sunk | while | flops 281147392 | bytes 17370192 | solution.py:158
  219.2 4.3 all-to-all-start.1
  223.7 18.0 %all-to-all-done.1 = bf16[4,512,256]{1,2,0:T(8,128)(2,1)} async-done(((bf16[4,512,256]{1,2,0:T(8,128)(2,1)}), bf16[4,512,256]{1,2,0:T(8,128)(2,1)}, u32[]{:S(2)}, u32[]{:S(2)}) %all-to-all-start.1) | async-done | bytes 1048608 | tf_op jit(solution)/shard_map/all_to_all | solution.py:159
  241.7 3.6 fusion.58
  247.0 27.2 %multiply_convert_fusion.1 = (bf16[512,4096]{1,0:T(8,128)(2,1)}, f32[512,4096]{1,0:T(8,128)}, f32[512,4096]{1,0:T(8,128)}) fusion(f32[4096]{0:T(1024)S(1)} %convert_element_type.170, bf16[4096,1024]{1,0:T(8,128)(2,1)} %all-gather.18.cloned.1.call-done, f32[512,1024]{1,0:T(8,128)} %copy-done, f32[1024]{0:T(1024)S(1)} %convert_element_type.168, ...), kind=kOutput, calls=%fused_computation.37 | convolution fusion | flops 4436000768 | bytes 31485952 | tf_op jit(solution)/shard_map/td,fd->tf/dot_general | solution.py:166
  274.2 10.3 %all-gather.20.cloned.1.call-done = bf16[4096,1024]{1,0:T(8,128)(2,1)} async-done(((bf16[1024,1024]{1,0:T(8,128)(2,1)}), bf16[4096,1024]{1,0:T(8,128)(2,1)}) %all-gather.20.cloned.1.call-update) | async-done | bytes 8388624 | tf_op jit(solution)/shard_map/all_gather | solution.py:126
  284.5 10.0 fusion.59
  294.9 1.5 multiply_reduce_fusion.1
  296.4 2.0 fusion.50
  298.4 1.3 copy-done.7
  300.6 7.1 convolution_convert_fusion
  307.7 13.5 %convert_reduce_fusion = (f32[4096]{0:T(1024)S(1)}, bf16[512,4096]{1,0:T(8,128)(2,1)S(1)}) fusion(f32[512,4096]{1,0:T(8,128)} %get-tuple-element.209, f32[512,4096]{1,0:T(8,128)} %get-tuple-element.234, f32[4096]{0:T(1024)S(1)} %convert_element_type.170, bf16[512,1024]{1,0:T(8,128)(2,1)S(1)} %get-tuple-element.199, ...), kind=kOutput, calls=%fused_computation.35 | convolution fusion | flops 4330614784 | bytes 30441472 | tf_op jit(solution)/shard_map/td,fd->tf/dot_general | solution.py:185
  321.3 7.0 convolution_convert_fusion.1
  328.3 13.9 %pad_maximum_fusion = bf16[4096,2048]{0,1:T(8,128)(2,1)} fusion(bf16[4096,1024]{0,1:T(8,128)(2,1)} %convolution_convert_fusion, bf16[4096,1024]{0,1:T(8,128)(2,1)} %convolution_convert_fusion.1), kind=kLoop, calls=%fused_computation.31 | loop fusion | flops 33554432 | bytes 33554432 | tf_op jit(solution)/shard_map/concatenate | solution.py:223
  342.2 11.4 %multiply_reduce_fusion.2 = (f32[1024]{0:T(1024)S(1)}, f32[512]{0:T(512)S(1)}, f32[1024]{0:T(1024)S(1)}, f32[512,1024]{1,0:T(8,128)S(1)}) fusion(f32[512,1024]{1,0:T(8,128)} %copy-done, f32[512]{0:T(512)S(1)} %fusion.42, f32[512]{0:T(512)S(1)} %broadcast_multiply_fusion.1, f32[1024]{0:T(1024)S(1)} %convert_element_type.167, ...), kind=kOutput, calls=%fused_computation.61 | convolution fusion | flops 4300207616 | bytes 18894848 | tf_op jit(solution)/shard_map/dot_general | solution.py:187
  354.3 1.3 copy-done.5
  356.9 2.3 fusion.29
  359.2 6.2 copy.82
  365.9 9.0 reduce.7
  374.9 3.9 reshape.269
  378.8 4.3 all-to-all-start.2
  383.1 26.1 %all-to-all-done.2 = bf16[4,2,65536]{2,1,0:T(2,128)(2,1)} async-done(((bf16[4,2,65536]{2,1,0:T(2,128)(2,1)}), bf16[4,2,65536]{2,1,0:T(2,128)(2,1)}, u32[]{:S(2)}, u32[]{:S(2)}) %all-to-all-start.2) | async-done | bytes 1048608 | tf_op jit(solution)/shard_map/all_to_all | solution.py:193
  409.2 4.0 reshape.270
  413.2 2.8 copy.95
  416.1 35.0 %while.23 = (s32[]{:T(128)}, bf16[4,512,3,256]{1,3,2,0:T(8,128)(2,1)}, bf16[4,512,3,256]{1,3,2,0:T(8,128)(2,1)S(1)}, pred[4,512]{1,0:T(4,128)(4,1)S(1)}, f32[4,4...) while((s32[]{:T(128)}, bf16[4,512,3,256]{1,3,2,0:T(8,128)(2,1)}, ...), condition=%wide.region_14.15_spmd, body=%wide.region_12.14_spmd.sunk | while | flops 689829888 | bytes 39382108 | solution.py:200
  418.6 1.5 multiply_reduce_fusion.8
  420.1 1.4 multiply_convert_fusion.5
  427.4 1.5 multiply_reduce_fusion.8
  428.9 1.4 multiply_convert_fusion.5
  436.1 1.5 multiply_reduce_fusion.8
  437.6 1.4 multiply_convert_fusion.5
  444.9 1.5 multiply_reduce_fusion.8
  446.4 1.4 multiply_convert_fusion.5
  451.1 3.8 all-to-all-start.3
  455.0 4.2 convolution_convert_fusion.3
  459.2 51.5 %all-to-all-done.3 = bf16[4,512,3,256]{1,3,2,0:T(8,128)(2,1)S(1)} async-done(((bf16[4,512,3,256]{1,3,2,0:T(8,128)(2,1)}), bf16[4,512,3,256]{1,3,2,0:T(8,128)(2,1)S(1)}, u32[]{:S(2)}, u32[]{:S(2)}) %all-to-all-start.3) | async-done | bytes 3145760 | tf_op jit(solution)/shard_map/all_to_all | solution.py:201
  510.9 2.4 copy-done.35
  517.1 2.5 fusion.57
  520.0 4.0 convolution_convert_fusion.2
  524.0 9.9 pad_maximum_fusion.1
  534.0 6.8 fusion.55
  540.8 2.2 copy-done.4
  543.0 1.6 fusion.56
  544.6 1.9 copy.84
  546.5 1.8 copy.86
  548.6 41.3 %all-reduce = (f32[1024]{0:T(1024)}, f32[1024]{0:T(1024)}, f32[1024]{0:T(1024)}, f32[1024]{0:T(1024)}, f32[4096]{0:T(1024)}, /*index=5*/f32[1024]{0:T(1024)}, f3...) all-reduce(f32[1024]{0:T(1024)S(1)} %get-tuple-element.240, ...), channel_id=1, replica_groups=mesh['dp'=8,'seq'=4] {'dp','seq'}, use_global_device_ids=true, to_apply=%region_22.23 | all-reduce | flops 13312 | bytes 104448 | tf_op jit(solution)/shard_map/psum | solution.py:252
  589.9 29.4 %reduce-scatter.3.cloned.1.call-done = bf16[256,5120]{1,0:T(8,128)(2,1)} async-done(((bf16[1024,5120]{1,0:T(8,128)(2,1)}), bf16[256,5120]{1,0:T(8,128)(2,1)}) %reduce-scatter.3.cloned.1.call-update) | async-done | bytes 2621456 | tf_op jit(solution)/shard_map/reduce_scatter | solution.py:234
  619.3 267.7 %all-reduce.6 = f32[256,5120]{1,0:T(8,128)} all-reduce(bf16[256,5120]{1,0:T(8,128)(2,1)} %reduce-scatter.3.cloned.1.call-done), channel_id=1, replica_groups=mesh['dp'=8,'seq'=4] {'dp'}, use_global_device_ids=true, to_apply=%region_17.18 | all-reduce | flops 1310720 | bytes 7864320 | tf_op jit(solution)/shard_map/psum | solution.py:240
  887.0 5.0 fusion.54
  892.0 114.9 %all-reduce.5.cloned.1.call-done = (f32[1024,1024]{0,1:T(8,128)}, f32[1024,1024]{0,1:T(8,128)}) async-done(((f32[1024,1024]{0,1:T(8,128)}, f32[1024,1024]{0,1:T(8,128)}), (f32[1024,1024]{0,1:T(8,128)}, f32[1024,1024]{0,1:T(8,128)})) %all-reduce.5.cloned.1.call-update) | async-done | bytes 8388624 | tf_op jit(solution)/shard_map/psum | solution.py:240
  1006.9 5.3 copy.88
  1012.3 5.3 copy.89
  (210 shorter events, 55.0 us)
Async XLA Ops:
  7.2 4.0 copy-start.25
  7.2 4.0 copy-start.26
  7.2 27.7 %copy-start.22 = (bf16[1,1024]{1,0:T(2,128)(2,1)S(1)}, bf16[1,1024]{1,0:T(2,128)(2,1)}, u32[]{:S(2)}) copy-start(bf16[1,1024]{1,0:T(2,128)(2,1)} %param.26) | copy-start | bytes 6148
  7.2 29.7 %copy-start.27 = (bf16[1024]{0:T(1024)(128)(2,1)S(1)}, bf16[1024]{0:T(1024)(128)(2,1)}, u32[]{:S(2)}) copy-start(bf16[1024]{0:T(1024)(128)(2,1)} %param.39) | copy-start | bytes 6148
  7.2 51.9 %copy-start.12 = (bf16[512,1024]{1,0:T(8,128)(2,1)S(1)}, bf16[512,1024]{1,0:T(8,128)(2,1)}, u32[]{:S(2)}) copy-start(bf16[512,1024]{1,0:T(8,128)(2,1)} %param.25) | copy-start | bytes 3145732
  7.2 27.7 %all-gather.8.cloned.1.call-start = ((), (), s32[]{:S(2)}) async-start(), calls=%async_computation.6 | async-start | bytes 2621440 | tf_op jit(solution)/shard_map/all_gather | solution.py:124
  8.0 51.1 %all-gather.12.cloned.1.call-start = ((), (), s32[]{:S(2)}) async-start(), calls=%async_computation.8 | async-start | bytes 2621440 | tf_op jit(solution)/shard_map/all_gather | solution.py:121
  8.7 74.5 %all-gather.10.cloned.1.call-start = ((), (), s32[]{:S(2)}) async-start(), calls=%async_computation.7 | async-start | bytes 2621440 | tf_op jit(solution)/shard_map/all_gather | solution.py:120
  9.5 97.8 %all-gather.14.cloned.1.call-start = ((), (), s32[]{:S(2)}) async-start(), calls=%async_computation.9 | async-start | bytes 2621440 | tf_op jit(solution)/shard_map/all_gather | solution.py:122
  10.0 213.6 %all-gather.16.cloned.1.call-start = ((), (), s32[]{:S(2)}) async-start(), calls=%async_computation.10 | async-start | bytes 2621440 | tf_op jit(solution)/shard_map/all_gather | solution.py:123
  10.6 236.4 %all-gather.18.cloned.1.call-start = ((), (), s32[]{:S(2)}) async-start(), calls=%async_computation.11 | async-start | bytes 10485760 | tf_op jit(solution)/shard_map/all_gather | solution.py:125
  36.9 204.8 %copy-start.16 = (f32[1024]{0:T(1024)}, f32[1024]{0:T(1024)S(1)}, u32[]{:S(2)}) copy-start(f32[1024]{0:T(1024)S(1)} %convert_add_fusion.1) | copy-start | bytes 12292
  107.3 3.0 copy-start.14
  107.3 3.0 copy-start.15
  116.3 5.8 copy-start.37
  116.3 83.5 %all-to-all-start = ((bf16[1,512,3,1024]{1,2,0,3:T(4,128)(2,1)}), bf16[1,512,3,1024]{1,2,0,3:T(4,128)(2,1)}, u32[]{:S(2)}, u32[]{:S(2)}) async-start(bf16[1,512,3,1024]{1,2,0,3:T(4,128)(2,1)} %copy.80), calls=%async_computation | async-start | bytes 8388608 | tf_op jit(solution)/shard_map/all_to_all | solution.py:157
  121.4 163.1 %all-gather.20.cloned.1.call-start = ((), (), s32[]{:S(2)}) async-start(), calls=%async_computation.12 | async-start | bytes 10485760 | tf_op jit(solution)/shard_map/all_gather | solution.py:126
  202.8 20.7 %copy-start.28 = (bf16[1024]{0:T(1024)(128)(2,1)S(1)}, bf16[1024]{0:T(1024)(128)(2,1)}, u32[]{:S(2)}) copy-start(bf16[1024]{0:T(1024)(128)(2,1)} %param.38) | copy-start | bytes 6148
  202.8 20.7 %copy-start.29 = (bf16[1024]{0:T(1024)(128)(2,1)S(1)}, bf16[1024]{0:T(1024)(128)(2,1)}, u32[]{:S(2)}) copy-start(bf16[1024]{0:T(1024)(128)(2,1)} %param.42) | copy-start | bytes 6148
  202.8 20.7 %copy-start.30 = (bf16[1024]{0:T(1024)(128)(2,1)S(1)}, bf16[1024]{0:T(1024)(128)(2,1)}, u32[]{:S(2)}) copy-start(bf16[1024]{0:T(1024)(128)(2,1)} %param.43) | copy-start | bytes 6148
  202.8 20.7 %copy-start.24 = (bf16[4096]{0:T(1024)(128)(2,1)S(1)}, bf16[4096]{0:T(1024)(128)(2,1)}, u32[]{:S(2)}) copy-start(bf16[4096]{0:T(1024)(128)(2,1)} %param.40) | copy-start | bytes 24580
  202.8 20.7 %copy-start.31 = (bf16[1024]{0:T(1024)(128)(2,1)S(1)}, bf16[1024]{0:T(1024)(128)(2,1)}, u32[]{:S(2)}) copy-start(bf16[1024]{0:T(1024)(128)(2,1)} %param.41) | copy-start | bytes 6148
  202.9 20.7 %copy-start.32 = (bf16[1024]{0:T(1024)(128)(2,1)S(1)}, bf16[1024]{0:T(1024)(128)(2,1)}, u32[]{:S(2)}) copy-start(bf16[1024]{0:T(1024)(128)(2,1)} %param.44) | copy-start | bytes 6148
  202.9 20.7 %copy-start.33 = (bf16[1024]{0:T(1024)(128)(2,1)S(1)}, bf16[1024]{0:T(1024)(128)(2,1)}, u32[]{:S(2)}) copy-start(bf16[1024]{0:T(1024)(128)(2,1)} %param.45) | copy-start | bytes 6148
  219.2 4.3 copy-start.18
  219.2 22.5 %all-to-all-start.1 = ((bf16[4,512,256]{1,2,0:T(8,128)(2,1)}), bf16[4,512,256]{1,2,0:T(8,128)(2,1)}, u32[]{:S(2)}, u32[]{:S(2)}) async-start(bf16[4,512,256]{1,2,0:T(8,128)(2,1)} %get-tuple-element.79), calls=%async_computation.1 | async-start | bytes 2097152 | tf_op jit(solution)/shard_map/all_to_all | solution.py:159
  223.4 310.5 %reduce-scatter.5.cloned.1.call-start = ((), (), s32[]{:S(2)}) async-start(), calls=%async_computation.14 | async-start | bytes 20971520 | tf_op jit(solution)/shard_map/reduce_scatter | solution.py:222
  245.3 1.3 copy-start
  284.5 10.3 %copy-start.8 = (bf16[512,1024]{1,0:T(8,128)(2,1)S(1)}, bf16[512,1024]{1,0:T(8,128)(2,1)}, u32[]{:S(2)}) copy-start(bf16[512,1024]{1,0:T(8,128)(2,1)} %param.28) | copy-start | bytes 3145732
  296.4 4.2 copy-start.38
  298.4 1.3 copy-start.7
  307.7 13.5 %copy-start.1 = (f32[512,1024]{1,0:T(8,128)S(1)}, f32[512,1024]{1,0:T(8,128)}, u32[]{:S(2)}) copy-start(f32[512,1024]{1,0:T(8,128)} %copy-done) | copy-start | bytes 6291460
  321.2 7.0 copy-start.39
  342.2 11.4 %copy-start.2 = (f32[512,1024]{1,0:T(8,128)S(1)}, f32[512,1024]{1,0:T(8,128)}, u32[]{:S(2)}) copy-start(f32[512,1024]{1,0:T(8,128)} %copy-done) | copy-start | bytes 6291460
  353.6 3.3 copy-start.10
  354.3 1.3 copy-start.5
  355.9 1.0 copy-start.11
  378.8 30.4 %all-to-all-start.2 = ((bf16[4,2,65536]{2,1,0:T(2,128)(2,1)}), bf16[4,2,65536]{2,1,0:T(2,128)(2,1)}, u32[]{:S(2)}, u32[]{:S(2)}) async-start(bf16[4,2,65536]{2,1,0:T(2,128)(2,1)} %reshape.269), calls=%async_computation.2 | async-start | bytes 2097152 | tf_op jit(solution)/shard_map/all_to_all | solution.py:193
  451.1 3.9 copy-start.23
  451.1 59.6 %all-to-all-start.3 = ((bf16[4,512,3,256]{1,3,2,0:T(8,128)(2,1)}), bf16[4,512,3,256]{1,3,2,0:T(8,128)(2,1)S(1)}, u32[]{:S(2)}, u32[]{:S(2)}) async-start(bf16[4,512,3,256]{1,3,2,0:T(8,128)(2,1)} %get-tuple-element.81), calls=%async_computation.3 | async-start | bytes 6291456 | tf_op jit(solution)/shard_map/all_to_all | solution.py:201
  454.9 164.4 %reduce-scatter.3.cloned.1.call-start = ((), (), s32[]{:S(2)}) async-start(), calls=%async_computation.13 | async-start | bytes 13107200 | tf_op jit(solution)/shard_map/reduce_scatter | solution.py:234
  510.6 2.6 copy-start.35
  510.9 9.1 copy-start.3
  513.3 1.6 copy-start.34
  514.8 1.6 copy-start.6
  514.9 2.2 copy-start.36
  517.1 2.9 copy-start.13
  517.1 2.9 copy-start.17
  520.0 4.0 copy-start.9
  533.9 473.0 %all-reduce.5.cloned.1.call-start = ((), (), s32[]{:S(2)}) async-start(), calls=%async_computation.15 | async-start | bytes 16777216 | tf_op jit(solution)/shard_map/psum | solution.py:240
  540.8 2.3 copy-start.4
  544.6 4.0 copy-start.19
  544.6 4.0 copy-start.20
  544.6 4.0 copy-start.21
Sparse Core Ops, SparseCore 0:
  9.6 25.2 all-gather.7
  36.5 22.5 all-gather.11
  60.7 22.5 all-gather.9
  84.7 22.5 all-gather.13
  108.7 27.7 all-gather.15
  137.9 83.4 all-gather.17
  223.0 61.5 all-gather.19
  342.3 155.0 reduce-scatter.4
  534.0 85.2 reduce-scatter.2
  624.4 382.4 all-reduce.4
where the time goes:
time: 1030 us; the launch traced here: 1020 us
  waiting for transfers between devices  419 us (41%)
  blocking collectives  309 us (30%)
  matrix products  135 us (13%)
  local copies, waits for them, and re-layouts  75.6 us (7%)
  other arithmetic  52.9 us (5%)
  starting transfers between devices  17.8 us (2%)
  between operations  15.3 us (1%)
    psum x1, blocking collectives, local(): lax.psum((share_in, share_down, attn_share), 'dp')  268 us
    psum x1, waiting for transfers between devices, local(): lax.psum((share_in, share_down, attn_share), 'dp')  115 us
    all_to_all x1, waiting for transfers between devices, local(): lax.all_to_all(stacked, 'seq', split_axis=3, concat_axis=0, tiled=True)  77.5 us
    all_to_all x1, waiting for transfers between devices, local(): lax.all_to_all(grad_stack, 'seq', split_axis=0, concat_axis=3, tiled=True)  51.5 us
    psum x1, blocking collectives, local(): lax.psum((jnp.sum(grad_query_rows, axis=0, dtype=jnp.float32), jnp.sum(gr...  41.3 us
    unnamed x86, local copies, waits for them, and re-layouts  32.8 us
    reduce_scatter x1, waiting for transfers between devices, local(): lax.psum_scatter(jnp.concatenate([term_qkv, term_out, term_time], axis=1)...  29.4 us
    dot_general x1, matrix products, local(): jnp.einsum('td,fd->tf', first_low, full_in, preferred_element_type=jnp.fl...  27.2 us
  transfers between devices with their start and end apart: 14, of which 11 were waited for; matrix products, arithmetic and copies ran while one was open for 18% of the time, Pallas kernels for 0%

commit v1 on v0

v1 whole, which is shorter than its diff:
```python
import jax
import jax.numpy as jnp
from jax import lax
from jax.sharding import PartitionSpec as P

HEAD_DIM = 64
BLOCK = 25


norm_eps = 1e-05
neg_large = -1e30


def layer_norm(values, gain, shift):
    center = values - jnp.mean(values, axis=-1, keepdims=True)
    spread = lax.rsqrt(jnp.mean(center * center, axis=-1, keepdims=True) + norm_eps)
    return center * spread * gain + shift


def exact_gelu(values):
    return jax.nn.gelu(values, approximate=False)


def split_heads(rows):
    return rows.reshape(rows.shape[0], rows.shape[1] // HEAD_DIM, HEAD_DIM)


def item_scores(queries, keys, key_valid):
    scores = jnp.einsum(
        "qhd,khd->hqk", split_heads(queries), split_heads(keys), preferred_element_type=jnp.float32
    ) * HEAD_DIM ** (-0.5)
    return jnp.where(key_valid[None, None, :], scores, neg_large)


def attend_forward(queries, keys, values, key_valid):
    masked = item_scores(queries, keys, key_valid)
    row_max = jnp.max(masked, axis=-1, keepdims=True)
    exp_scores = jnp.exp(masked - row_max)
    row_total = jnp.sum(exp_scores, axis=-1, keepdims=True)
    soft = (exp_scores / row_total).astype(jnp.bfloat16)
    mixed = jnp.einsum(
        "hqk,khd->qhd", soft, split_heads(values), preferred_element_type=jnp.float32
    )
    log_total = row_max[:, :, 0] + jnp.log(row_total[:, :, 0])
    return mixed.reshape(queries.shape).astype(jnp.bfloat16), log_total


def attend_backward(queries, keys, values, key_valid, log_total, grad_mixed):
    masked = item_scores(queries, keys, key_valid)
    soft = jnp.exp(masked - log_total[:, :, None])
    grad_heads = split_heads(grad_mixed)
    grad_value = jnp.einsum(
        "hqk,qhd->khd", soft.astype(jnp.bfloat16), grad_heads, preferred_element_type=jnp.float32
    )
    grad_soft = jnp.einsum(
        "qhd,khd->hqk", grad_heads, split_heads(values), preferred_element_type=jnp.float32
    )
    grad_scores = soft * (grad_soft - jnp.sum(soft * grad_soft, axis=-1, keepdims=True))
    scores_low = grad_scores.astype(jnp.bfloat16)
    scale = HEAD_DIM ** (-0.5)
    grad_query = scale * jnp.einsum(
        "hqk,khd->qhd", scores_low, split_heads(keys), preferred_element_type=jnp.float32
    )
    grad_key = scale * jnp.einsum(
        "hqk,qhd->khd", scores_low, split_heads(queries), preferred_element_type=jnp.float32
    )
    return tuple(
        grad.reshape(queries.shape).astype(jnp.bfloat16)
        for grad in (grad_query, grad_key, grad_value)
    )


def per_item(fn, item_count, slot_count, *arrays):
    if item_count == 1:
        return fn(*[a[0] for a in arrays])
    outs = lax.map(lambda packed: fn(*packed), arrays)
    return outs


def local(
    tokens,
    time_embed,
    lengths,
    cotangent,
    w_query,
    w_key,
    w_value,
    w_out,
    w_time,
    w_in,
    w_down,
    b_query,
    b_value,
    b_out,
    b_time,
    b_in,
    b_down,
    gain_one,
    shift_one,
    gain_two,
    shift_two,
):
    f32, bf16 = jnp.float32, jnp.bfloat16
    seq_rank = lax.axis_index("seq")
    item_count = time_embed.shape[0]
    token_count = tokens.shape[0]
    slot_count = token_count // item_count
    width = tokens.shape[1]
    rows = w_time.shape[0]

    def mm(a, b, dims):
        return lax.dot_general(a, b, (dims, ((), ())), preferred_element_type=f32)

    def gather(a):
        return lax.all_gather(a, "seq", axis=0, tiled=True)

    def scatter_sum(a):
        return lax.psum_scatter(a, "seq", scatter_dimension=0, tiled=True)

    full_time, full_query, full_key, full_value, full_out = (
        gather(w_time),
        gather(w_query),
        gather(w_key),
        gather(w_value),
        gather(w_out),
    )
    own_lengths = lax.dynamic_slice_in_dim(lengths, seq_rank * item_count, item_count, 0)
    slot_index = lax.broadcasted_iota(jnp.int32, (item_count, slot_count), 1)
    own_valid = slot_index < own_lengths[:, None] + BLOCK
    row_keep = own_valid.reshape(token_count, 1).astype(f32)
    time_proj = mm(time_embed, full_time, ((1,), (0,))) + b_time.astype(f32)
    resid = (tokens.reshape(item_count, slot_count, width) + time_proj[:, None, :]).reshape(
        token_count, width
    )
    resid_low = resid.astype(bf16)
    query_rows = (mm(resid_low, full_query, ((1,), (0,))) + b_query.astype(f32)).astype(bf16)
    key_rows = mm(resid_low, full_key, ((1,), (0,))).astype(bf16)
    value_rows = (mm(resid_low, full_value, ((1,), (0,))) + b_value.astype(f32)).astype(bf16)

    def split_items(a):
        return a.reshape(item_count, slot_count, -1)

    qkv = [split_items(a) for a in (query_rows, key_rows, value_rows)]
    mixed, log_total = per_item(attend_forward, item_count, slot_count, *qkv, own_valid)
    mixed_rows = mixed.reshape(token_count, width)
    attn_out = mm(mixed_rows, full_out, ((1,), (0,))) + b_out.astype(f32)
    first_norm, first_pull = jax.vjp(
        layer_norm, resid + attn_out, gain_one.astype(f32), shift_one.astype(f32)
    )
    first_group = gather(first_norm.astype(bf16))
    bias_in = lax.dynamic_slice_in_dim(b_in, seq_rank * w_in.shape[0], w_in.shape[0], 0)
    hidden_pre = mm(first_group, w_in, ((1,), (1,))) + bias_in.astype(f32)
    hidden, gelu_pull = jax.vjp(exact_gelu, hidden_pre)
    hidden_low = hidden.astype(bf16)
    ffn_part = mm(hidden_low, w_down, ((1,), (0,))).astype(bf16)
    ffn_out = scatter_sum(ffn_part).astype(f32) + b_down.astype(f32)
    second_norm, second_pull = jax.vjp(
        layer_norm, first_norm + ffn_out, gain_two.astype(f32), shift_two.astype(f32)
    )
    layer_out = (second_norm * row_keep).astype(bf16)
    grad_second_in, grad_gain_two, grad_shift_two = second_pull(cotangent.astype(f32) * row_keep)
    grad_ffn = grad_second_in.astype(bf16)
    grad_group = gather(grad_ffn)
    grad_hidden = mm(grad_group, w_down, ((1,), (1,)))
    grad_pre = gelu_pull(grad_hidden)[0].astype(bf16)
    back_part = mm(grad_pre, w_in, ((1,), (0,))).astype(bf16)
    grad_first = grad_second_in + scatter_sum(back_part).astype(f32)
    term_in = mm(grad_pre, first_group, ((0,), (0,))).astype(bf16)
    term_down = mm(hidden_low, grad_group, ((0,), (0,))).astype(bf16)
    sum_ffn = lax.psum(jnp.concatenate([term_in, term_down], axis=0), "dp").astype(f32)
    grad_first_in, grad_gain_one, grad_shift_one = first_pull(grad_first)
    grad_attn = grad_first_in.astype(bf16)
    grad_mixed = mm(grad_attn, full_out, ((1,), (1,))).astype(bf16)
    if item_count == 1:
        extra = (log_total[None], split_items(grad_mixed))
    else:
        extra = (log_total, split_items(grad_mixed))
    grad_query, grad_key, grad_value = (
        a.reshape(token_count, width)
        for a in per_item(attend_backward, item_count, slot_count, *qkv, own_valid, *extra)
    )
    grad_resid = (
        grad_first_in
        + mm(grad_query, full_query, ((1,), (1,)))
        + mm(grad_key, full_key, ((1,), (1,)))
        + mm(grad_value, full_value, ((1,), (1,)))
    )
    grad_tokens = grad_resid.astype(bf16)
    grad_time = jnp.sum(grad_resid.reshape(item_count, slot_count, width), axis=1).astype(bf16)
    terms = [
        mm(resid_low, grad_query, ((0,), (0,))),
        mm(resid_low, grad_key, ((0,), (0,))),
        mm(resid_low, grad_value, ((0,), (0,))),
        mm(mixed_rows, grad_attn, ((0,), (0,))),
    ]
    group = w_out.shape[0]
    stacked = jnp.stack([t.astype(bf16).reshape(-1, group, width) for t in terms], axis=1)
    share = scatter_sum(stacked.reshape(-1, width))
    sum_attn = lax.psum(share, "dp").astype(f32)
    small = jnp.concatenate(
        [
            jnp.stack(
                [
                    jnp.sum(grad_query, axis=0, dtype=f32),
                    jnp.sum(grad_value, axis=0, dtype=f32),
                    jnp.sum(grad_attn, axis=0, dtype=f32),
                    jnp.sum(grad_ffn, axis=0, dtype=f32),
                    grad_gain_one,
                    grad_shift_one,
                    grad_gain_two,
                    grad_shift_two,
                ]
            ).astype(bf16),
            jnp.sum(grad_pre, axis=0, dtype=f32).reshape(-1, width).astype(bf16),
            time_embed,
            grad_time,
        ],
        axis=0,
    )
    every = lax.all_gather(small, ("dp", "seq"), axis=0)
    vectors = jnp.sum(every[:, :8], axis=0, dtype=f32)
    hidden_rows = every.shape[1] - 8 - 2 * item_count
    in_parts = every[:, 8 : 8 + hidden_rows].reshape(-1, b_in.shape[0])
    grad_b_in = jnp.sum(in_parts, axis=0, dtype=f32)
    time_rows = every[:, 8 + hidden_rows : 8 + hidden_rows + item_count].reshape(-1, width)
    time_grads = every[:, 8 + hidden_rows + item_count :].reshape(-1, width)
    own_columns = lax.dynamic_slice_in_dim(time_rows, seq_rank * rows, rows, 1)
    grad_w_time = mm(own_columns, time_grads, ((0,), (0,)))
    grad_b_time = jnp.sum(time_grads, axis=0, dtype=f32)
    return (
        layer_out,
        grad_tokens,
        sum_attn[:group],
        sum_attn[group : 2 * group],
        sum_attn[2 * group : 3 * group],
        sum_attn[3 * group :],
        grad_w_time,
        sum_ffn[: w_in.shape[0]],
        sum_ffn[w_in.shape[0] :],
        vectors[0],
        vectors[1],
        vectors[2],
        grad_b_time,
        grad_b_in,
        vectors[3],
        vectors[4],
        vectors[5],
        vectors[6],
        vectors[7],
    )


def solution(mesh):
    in_specs = (
        P(("dp", "seq"), None),
        P(("dp", "seq"), None),
        P("dp"),
        P(("dp", "seq"), None),
        P("seq", None),
        P("seq", None),
        P("seq", None),
        P("seq", None),
        P("seq", None),
        P("seq", None),
        P("seq", None),
        P(),
        P(),
        P(),
        P(),
        P(),
        P(),
        P(),
        P(),
        P(),
        P(),
    )
    out_specs = (
        P(("dp", "seq"), None),
        P(("dp", "seq"), None),
        P("seq", None),
        P("seq", None),
        P("seq", None),
        P("seq", None),
        P("seq", None),
        P("seq", None),
        P("seq", None),
        P(),
        P(),
        P(),
        P(),
        P(),
        P(),
        P(),
        P(),
        P(),
        P(),
    )
    return jax.shard_map(local, mesh=mesh, in_specs=in_specs, out_specs=out_specs, check_vma=False)
```

time: 1030 us -> 741 us (0.72)
  blocking collectives: 309 us -> 51.7 us
  local copies, waits for them, and re-layouts: 75.6 us -> 35.2 us
  waiting for transfers between devices: 419 us -> 443 us
  starting transfers between devices: 17.8 us -> 1.27 us
    psum x2 -> x0, blocking collectives: 309 us -> none  [the longest x1 268 us: local(): lax.psum((share_in, share_down, attn_share), 'dp')]
    all_to_all x4 -> x0, waiting for transfers between devices: 173 us -> none  [the longest x1 77.5 us: local(): lax.all_to_all(stacked, 'seq', split_axis=3, concat_axis=0, tiled=True)]
    reduce_scatter x2 -> x3, waiting for transfers between devices: 29.4 us -> 145 us  [scatter_sum(): return lax.psum_scatter(a, 'seq', scatter_dimension=0, tiled=True)]
    all_gather x0 -> x1, blocking collectives: none -> 51.7 us  [local(): every = lax.all_gather(small, ('dp', 'seq'), axis=0)]
    psum x1, waiting for transfers between devices: 115 us -> 157 us  [local(): sum_attn = lax.psum(share, 'dp').astype(f32)]
    all_gather x7, waiting for transfers between devices: 96.8 us -> 138 us  [gather(): return lax.all_gather(a, 'seq', axis=0, tiled=True)]
    unnamed x86 -> x78, local copies, waits for them, and re-layouts: 32.8 us -> 9.91 us
    concatenate x2 -> x1, other arithmetic: 23.8 us -> 2.45 us  [local(): jnp.concatenate([term_in, term_down], axis=0)]
  transfers between devices with their start and end apart: 14 -> 11, of which waited for: 11 -> 11; matrix products, arithmetic and copies ran while one was open for 18% -> 10% of each run, Pallas kernels for 0% -> 0%
where the time goes in v1:
time: 741 us; the launch traced here: 732 us
  waiting for transfers between devices  443 us (60%)
  matrix products  138 us (19%)
  blocking collectives  51.7 us (7%)
  other arithmetic  47.2 us (6%)
  local copies, waits for them, and re-layouts  35.2 us (5%)
  between operations  15.6 us (2%)
    psum x1, waiting for transfers between devices, local(): sum_attn = lax.psum(share, 'dp').astype(f32)  157 us
    reduce_scatter x3, waiting for transfers between devices, scatter_sum(): return lax.psum_scatter(a, 'seq', scatter_dimension=0, tiled=True)  145 us
    all_gather x7, waiting for transfers between devices, gather(): return lax.all_gather(a, 'seq', axis=0, tiled=True)  138 us
    dot_general x20, matrix products, mm(): return lax.dot_general(a, b, (dims, ((), ())), preferred_element_type=f32)  96.6 us
    all_gather x1, blocking collectives, local(): every = lax.all_gather(small, ('dp', 'seq'), axis=0)  51.7 us
  transfers between devices with their start and end apart: 11, of which 11 were waited for; matrix products, arithmetic and copies ran while one was open for 10% of the time, Pallas kernels for 0%

profile of v1, /device:TPU:0, one launch (start us, length us, event | category | flops | bytes accessed | tf_op | source)
XLA Modules:
  0.0 732.2 jit_solution(3286179977434555433)
XLA Ops:
  8.0 0.7 all-gather.14.cloned.1.call-update
  10.6 1.2 dynamic_slice.11
  16.0 18.9 %all-gather.10.cloned.1.call-done = bf16[1024,1024]{1,0:T(8,128)(2,1)} async-done(((bf16[256,1024]{1,0:T(8,128)(2,1)}), bf16[1024,1024]{1,0:T(8,128)(2,1)}) %all-gather.10.cloned.1.call-update) | async-done | bytes 2097168 | tf_op jit(solution)/shard_map/all_gather | solution.py:115
  34.9 2.0 fusion.28
  36.9 22.1 %all-gather.14.cloned.1.call-done = bf16[1024,1024]{1,0:T(8,128)(2,1)} async-done(((bf16[256,1024]{1,0:T(8,128)(2,1)}), bf16[1024,1024]{1,0:T(8,128)(2,1)}) %all-gather.14.cloned.1.call-update) | async-done | bytes 2097168 | tf_op jit(solution)/shard_map/all_gather | solution.py:115
  59.1 3.2 add_convert_fusion.1
  62.2 1.3 copy.72
  63.6 19.7 %all-gather.16.cloned.1.call-done = bf16[1024,1024]{1,0:T(8,128)(2,1)} async-done(((bf16[256,1024]{1,0:T(8,128)(2,1)}), bf16[1024,1024]{1,0:T(8,128)(2,1)}) %all-gather.16.cloned.1.call-update) | async-done | bytes 2097168 | tf_op jit(solution)/shard_map/all_gather | solution.py:115
  83.2 4.1 convolution_convert_fusion.9
  87.4 1.5 copy.73
  88.9 9.2 %fusion.46 = (f32[16,512]{1,0:T(8,128)S(1)}, f32[16,512,512]{1,2,0:T(8,128)}) fusion(bf16[512,16,64]{0,2,1:T(8,128)(2,1)} %bitcast.89, bf16[512,16,64]{0,2,1:T(8,128)(2,1)S(1)} %bitcast.87, pred[512]{0:T(512)(128)(4,1)S(1)} %iota_compare_fusion), kind=kOutput, calls=%fused_computation.107 | convolution fusion | flops 549445632 | bytes 18907648 | tf_op jit(solution)/shard_map/qhd,khd->hqk/dot_general | solution.py:29
  98.0 9.2 %all-gather.12.cloned.1.call-done = bf16[1024,1024]{1,0:T(8,128)(2,1)} async-done(((bf16[256,1024]{1,0:T(8,128)(2,1)}), bf16[1024,1024]{1,0:T(8,128)(2,1)}) %all-gather.12.cloned.1.call-update) | async-done | bytes 2097168 | tf_op jit(solution)/shard_map/all_gather | solution.py:115
  107.2 4.1 add_convert_fusion.2
  111.4 1.5 copy.71
  112.9 9.4 %fusion = f32[16,512]{1,0:T(8,128)S(1)} fusion(f32[16,512,512]{1,2,0:T(8,128)} %get-tuple-element.61, f32[16,512]{1,0:T(8,128)S(1)} %get-tuple-element.60), kind=kLoop, calls=%fused_computation.6 | loop fusion | flops 8380416 | bytes 16842752 | tf_op jit(solution)/shard_map/reduce_sum | solution.py:39
  122.2 8.5 %fusion.16 = bf16[16,64,512]{2,1,0:T(8,128)(2,1)} fusion(bf16[512,16,64]{0,2,1:T(8,128)(2,1)S(1)} %bitcast.93, f32[16,512,512]{1,2,0:T(8,128)} %get-tuple-element.61, f32[16,512]{1,0:T(8,128)S(1)} %fusion, f32[16,512]{1,0:T(8,128)S(1)} %get-tuple-element.60), kind=kOutput, calls=%fused_computation.64 | convolution fusion | flops 549978112 | bytes 18939904 | tf_op jit(solution)/shard_map/hqk,khd->qhd/dot_general | solution.py:41
  131.2 3.6 fusion.47
  135.2 0.9 copy-done.1
  136.1 1.4 fusion.15
  137.8 0.7 dynamic-slice_convert_fusion
  138.5 33.7 %all-gather.20.cloned.1.call-done = bf16[2048,1024]{1,0:T(8,128)(2,1)} async-done(((bf16[512,1024]{1,0:T(8,128)(2,1)}), bf16[2048,1024]{1,0:T(8,128)(2,1)}) %all-gather.20.cloned.1.call-update) | async-done | bytes 4194320 | tf_op jit(solution)/shard_map/all_gather | solution.py:115
  172.1 25.7 %multiply_convert_fusion.1 = (bf16[2048,1024]{1,0:T(8,128)(2,1)S(1)}, f32[2048,1024]{1,0:T(8,128)}, f32[2048,1024]{1,0:T(8,128)}) fusion(f32[1024]{0:T(1024)S(1)} %dynamic-slice_convert_fusion, bf16[2048,1024]{1,0:T(8,128)(2,1)} %all-gather.20.cloned.1.call-done, bf16[1024,1024]{1,0:T(8,128)(2,1)S(1)} %copy-done), kind=kOutput, calls=%fused_computation.14 | convolution fusion | flops 4433379328 | bytes 27267072 | tf_op jit(solution)/shard_map/dot_general | solution.py:112
  197.8 2.0 copy-done.36
  199.8 6.0 convolution_convert_fusion.1
  206.6 44.0 %reduce-scatter.4.cloned.1.call-done = bf16[512,1024]{1,0:T(8,128)(2,1)} async-done(((bf16[2048,1024]{1,0:T(8,128)(2,1)}), bf16[512,1024]{1,0:T(8,128)(2,1)}) %reduce-scatter.4.cloned.1.call-update) | async-done | bytes 1048592 | tf_op jit(solution)/shard_map/reduce_scatter | solution.py:118
  250.6 2.7 fusion.39
  253.6 1.0 multiply_reduce_fusion.1
  254.6 2.0 fusion.38
  256.6 1.3 copy-done.3
  258.0 1.2 fusion.35
  259.6 34.2 %all-gather.22.cloned.1.call-done = bf16[2048,1024]{1,0:T(8,128)(2,1)} async-done(((bf16[512,1024]{1,0:T(8,128)(2,1)}), bf16[2048,1024]{1,0:T(8,128)(2,1)}) %all-gather.22.cloned.1.call-update) | async-done | bytes 4194320 | tf_op jit(solution)/shard_map/all_gather | solution.py:115
  293.8 13.3 %fusion.34 = (bf16[1024]{0:T(1024)(128)(2,1)S(1)}, bf16[2048,1024]{1,0:T(8,128)(2,1)S(1)}) fusion(f32[2048,1024]{1,0:T(8,128)} %get-tuple-element.40, f32[2048,1024]{1,0:T(8,128)} %get-tuple-element.64, f32[1024]{0:T(1024)S(1)} %dynamic-slice_convert_fusion, bf16[2048,1024]{1,0:T(8,128)(2,1)} %all-gather.22.cloned.1.call-done, bf16[1024,1024]{1,0:T(8,128)(2,1)} %param.31), kind=kOutput, calls=%fused_computation.96 | convolution fusion | flops 4328520704 | bytes 27269120 | tf_op jit(solution)/shard_map/dot_general | solution.py:112
  307.2 1.9 copy-done.37
  309.1 6.0 convolution_convert_fusion
  315.2 44.7 %reduce-scatter.6.cloned.1.call-done = bf16[512,1024]{1,0:T(8,128)(2,1)} async-done(((bf16[2048,1024]{1,0:T(8,128)(2,1)}), bf16[512,1024]{1,0:T(8,128)(2,1)}) %reduce-scatter.6.cloned.1.call-update) | async-done | bytes 1048592 | tf_op jit(solution)/shard_map/reduce_scatter | solution.py:118
  359.8 3.7 multiply_reduce_fusion.2
  363.9 0.9 fusion.37
  365.1 1.0 copy-done.8
  366.5 2.3 convolution_convert_fusion.8
  368.7 1.5 copy.75
  370.2 11.4 %multiply_reduce_fusion = (f32[16,512]{1,0:T(8,128)S(1)}, f32[16,512,512]{1,2,0:T(8,128)}) fusion(f32[16,512,512]{1,2,0:T(8,128)} %get-tuple-element.61, f32[16,512]{1,0:T(8,128)S(1)} %log_add_fusion, bf16[512,16,64]{0,2,1:T(8,128)(2,1)S(1)} %bitcast.91, bf16[512,16,64]{0,2,1:T(8,128)(2,1)} %bitcast.94), kind=kOutput, calls=%fused_computation.1 | convolution fusion | flops 549445632 | bytes 35717120 | tf_op jit(solution)/shard_map/qhd,khd->hqk/dot_general | solution.py:55
  381.6 12.0 %multiply_convert_fusion = bf16[16,512,512]{1,2,0:T(8,128)(2,1)S(1)} fusion(f32[16,512,512]{1,2,0:T(8,128)} %get-tuple-element.66, f32[16,512,512]{1,2,0:T(8,128)} %get-tuple-element.61, f32[16,512]{1,0:T(8,128)S(1)} %get-tuple-element.65, f32[16,512]{1,0:T(8,128)S(1)} %log_add_fusion), kind=kLoop, calls=%fused_computation | loop fusion | flops 16777216 | bytes 42008576 | tf_op jit(solution)/shard_map/convert_element_type | solution.py:59
  393.6 1.5 bitcast_reduce_fusion.1
  395.2 2.6 multiply_convert_fusion.2
  397.9 1.3 convolution_convert_fusion.4
  399.1 8.6 %bitcast_reduce_fusion = (bf16[16,64]{1,0:T(8,128)(2,1)S(1)}, bf16[16,64,512]{2,1,0:T(8,128)(2,1)S(1)}) fusion(bf16[512,16,64]{0,2,1:T(8,128)(2,1)S(1)} %bitcast.92, f32[16,512,512]{1,2,0:T(8,128)} %get-tuple-element.61, f32[16,512]{1,0:T(8,128)S(1)} %log_add_fusion), kind=kOutput, calls=%fused_computation.68 | convolution fusion | flops 546307072 | bytes 18909184 | tf_op jit(solution)/shard_map/hqk,qhd->khd/dot_general | solution.py:52
  407.8 1.3 convolution_convert_fusion.7
  409.1 1.3 convolution_convert_fusion.6
  410.5 1.3 convolution_convert_fusion.5
  411.8 3.8 pad_maximum_fusion
  415.6 7.9 %copy.79 = bf16[4,4,256,1024]{3,2,1,0:T(8,128)(2,1)} copy(bf16[4,4,256,1024]{3,2,0,1:T(8,128)(2,1)} %pad_maximum_fusion) | data formatting | bytes 16777216 | tf_op jit(solution)/shard_map/stack | solution.py:197
  423.9 8.2 %convolution_convert_fusion.2 = bf16[1024,1024]{1,0:T(8,128)(2,1)S(1)} fusion(bf16[2048,1024]{1,0:T(8,128)(2,1)} %copy-done.36, bf16[2048,1024]{1,0:T(8,128)(2,1)} %all-gather.22.cloned.1.call-done), kind=kOutput, calls=%fused_computation.57 | convolution fusion | flops 4296015872 | bytes 10485760 | tf_op jit(solution)/shard_map/dot_general | solution.py:112
  432.1 4.8 convolution_convert_fusion.3
  436.9 2.5 pad_maximum_fusion.1
  439.3 55.8 %reduce-scatter.8.cloned.1.call-done = bf16[1024,1024]{1,0:T(8,128)(2,1)} async-done(((bf16[4096,1024]{1,0:T(8,128)(2,1)}), bf16[1024,1024]{1,0:T(8,128)(2,1)}) %reduce-scatter.8.cloned.1.call-update) | async-done | bytes 2097168 | tf_op jit(solution)/shard_map/reduce_scatter | solution.py:118
  495.2 3.0 fusion.48
  498.3 1.3 fusion.49
  500.2 0.7 copy-done.35
  500.8 2.5 fusion.42
  503.7 51.7 %all-gather.1 = bf16[32,11,1024]{2,1,0:T(8,128)(2,1)S(1)} all-gather(bf16[1,11,1024]{2,1,0:T(8,128)(2,1)S(1)} %bitcast.107), channel_id=2, replica_groups=mesh['dp'=8,'seq'=4] {'dp','seq'}, dimensions={0}, use_global_device_ids=true | all-gather | bytes 743424 | tf_op jit(solution)/shard_map/all_gather | solution.py:220
  558.0 1.3 fusion.27
  559.3 156.8 %all-reduce.3.cloned.1.call-done = (bf16[1024,1024]{1,0:T(8,128)(2,1)}, bf16[2048,1024]{1,0:T(8,128)(2,1)}) async-done(((bf16[1024,1024]{1,0:T(8,128)(2,1)}, bf16[2048,1024]{1,0:T(8,128)(2,1)}), (bf16[1024,1024]{1,0:T(8,128)(2,1)}, bf16[2048,1024]{1,0:T(8,128)(2,1)})) %all-reduce.3.cloned.1.call-update) | async-done | bytes 6291472 | tf_op jit(solution)/shard_map/psum | solution.py:199
  716.2 6.8 fusion.41
  723.0 2.2 fusion.43
  (136 shorter events, 13.7 us)
Async XLA Ops:
  7.2 164.9 %copy-start = (bf16[1024,1024]{1,0:T(8,128)(2,1)S(1)}, bf16[1024,1024]{1,0:T(8,128)(2,1)}, u32[]{:S(2)}) copy-start(bf16[1024,1024]{1,0:T(8,128)(2,1)} %param.30) | copy-start | bytes 6291460
  7.2 29.7 %copy-start.28 = (bf16[1024]{0:T(1024)(128)(2,1)S(1)}, bf16[1024]{0:T(1024)(128)(2,1)}, u32[]{:S(2)}) copy-start(bf16[1024]{0:T(1024)(128)(2,1)} %param.35) | copy-start | bytes 6148
  7.2 27.7 %all-gather.10.cloned.1.call-start = ((), (), s32[]{:S(2)}) async-start(), calls=%async_computation.3 | async-start | bytes 2621440 | tf_op jit(solution)/shard_map/all_gather | solution.py:115
  7.9 51.1 %all-gather.14.cloned.1.call-start = ((), (), s32[]{:S(2)}) async-start(), calls=%async_computation.5 | async-start | bytes 2621440 | tf_op jit(solution)/shard_map/all_gather | solution.py:115
  8.7 74.5 %all-gather.16.cloned.1.call-start = ((), (), s32[]{:S(2)}) async-start(), calls=%async_computation.6 | async-start | bytes 2621440 | tf_op jit(solution)/shard_map/all_gather | solution.py:115
  9.4 97.8 %all-gather.12.cloned.1.call-start = ((), (), s32[]{:S(2)}) async-start(), calls=%async_computation.4 | async-start | bytes 2621440 | tf_op jit(solution)/shard_map/all_gather | solution.py:115
  10.0 121.2 %all-gather.18.cloned.1.call-start = ((), (), s32[]{:S(2)}) async-start(), calls=%async_computation.7 | async-start | bytes 2621440 | tf_op jit(solution)/shard_map/all_gather | solution.py:115
  10.6 161.5 %all-gather.20.cloned.1.call-start = ((), (), s32[]{:S(2)}) async-start(), calls=%async_computation.8 | async-start | bytes 5242880 | tf_op jit(solution)/shard_map/all_gather | solution.py:115
  36.9 94.3 %copy-start.25 = (f32[1024]{0:T(1024)}, f32[1024]{0:T(1024)S(1)}, u32[]{:S(2)}) copy-start(f32[1024]{0:T(1024)S(1)} %convert_add_fusion.2) | copy-start | bytes 12292
  88.9 9.2 %copy-start.5 = (bf16[512,1024]{0,1:T(8,128)(2,1)}, bf16[512,1024]{0,1:T(8,128)(2,1)S(1)}, u32[]{:S(2)}) copy-start(bf16[512,1024]{0,1:T(8,128)(2,1)S(1)} %copy.73) | copy-start | bytes 3145732
  112.9 9.4 %copy-start.11 = (bf16[512,1024]{0,1:T(8,128)(2,1)}, bf16[512,1024]{0,1:T(8,128)(2,1)S(1)}, u32[]{:S(2)}) copy-start(bf16[512,1024]{0,1:T(8,128)(2,1)S(1)} %copy.71) | copy-start | bytes 3145732
  134.8 1.3 copy-start.1
  137.5 113.1 %reduce-scatter.4.cloned.1.call-start = ((), (), s32[]{:S(2)}) async-start(), calls=%async_computation.9 | async-start | bytes 5242880 | tf_op jit(solution)/shard_map/reduce_scatter | solution.py:118
  172.1 27.7 %copy-start.33 = (bf16[1024,1024]{1,0:T(8,128)(2,1)S(1)}, bf16[1024,1024]{1,0:T(8,128)(2,1)}, u32[]{:S(2)}) copy-start(bf16[1024,1024]{1,0:T(8,128)(2,1)} %param.31) | copy-start | bytes 6291460
  197.8 2.0 copy-start.36
  205.8 0.7 copy-start.29
  205.8 0.7 copy-start.30
  205.8 0.7 copy-start.31
  205.9 47.8 %copy-start.12 = (bf16[512,1024]{1,0:T(8,128)(2,1)S(1)}, bf16[512,1024]{1,0:T(8,128)(2,1)}, u32[]{:S(2)}) copy-start(bf16[512,1024]{1,0:T(8,128)(2,1)} %param.24) | copy-start | bytes 3145732
  205.9 87.9 %all-gather.22.cloned.1.call-start = ((), (), s32[]{:S(2)}) async-start(), calls=%async_computation.10 | async-start | bytes 5242880 | tf_op jit(solution)/shard_map/all_gather | solution.py:115
  256.6 1.3 copy-start.3
  259.2 100.6 %reduce-scatter.6.cloned.1.call-start = ((), (), s32[]{:S(2)}) async-start(), calls=%async_computation.11 | async-start | bytes 5242880 | tf_op jit(solution)/shard_map/reduce_scatter | solution.py:118
  307.1 1.9 copy-start.37
  315.1 180.0 %reduce-scatter.8.cloned.1.call-start = ((), (), s32[]{:S(2)}) async-start(), calls=%async_computation.12 | async-start | bytes 10485760 | tf_op jit(solution)/shard_map/reduce_scatter | solution.py:118
  359.8 3.7 copy-start.2
  359.8 3.8 copy-start.4
  359.8 4.0 copy-start.13
  363.9 2.6 copy-start.16
  364.8 1.3 copy-start.8
  365.1 1.4 copy-start.19
  381.6 12.0 %copy-start.6 = (bf16[512,1024]{0,1:T(8,128)(2,1)S(1)}, bf16[512,1024]{0,1:T(8,128)(2,1)}, u32[]{:S(2)}) copy-start(bf16[512,1024]{0,1:T(8,128)(2,1)} %copy-done.5) | copy-start | bytes 3145732
  393.6 1.5 copy-start.7
  395.2 12.6 %copy-start.14 = (bf16[16,64,512]{2,1,0:T(8,128)(2,1)}, bf16[16,64,512]{2,1,0:T(8,128)(2,1)S(1)}, u32[]{:S(2)}) copy-start(bf16[16,64,512]{2,1,0:T(8,128)(2,1)S(1)} %get-tuple-element.69) | copy-start | bytes 3145732
  395.2 2.7 copy-start.20
  395.2 2.6 copy-start.22
  397.8 11.3 %copy-start.17 = (bf16[16,64,512]{2,1,0:T(8,128)(2,1)}, bf16[16,64,512]{2,1,0:T(8,128)(2,1)S(1)}, u32[]{:S(2)}) copy-start(bf16[16,64,512]{2,1,0:T(8,128)(2,1)S(1)} %multiply_convert_fusion.2) | copy-start | bytes 3145732
  399.1 8.7 %copy-start.21 = (bf16[512,1024]{1,0:T(8,128)(2,1)S(1)}, bf16[512,1024]{1,0:T(8,128)(2,1)}, u32[]{:S(2)}) copy-start(bf16[512,1024]{1,0:T(8,128)(2,1)} %param.21) | copy-start | bytes 3145732
  399.1 8.7 %copy-start.26 = (f32[1024]{0:T(1024)S(1)}, f32[1024]{0:T(1024)}, u32[]{:S(2)}) copy-start(f32[1024]{0:T(1024)} %copy-done.25) | copy-start | bytes 12292
  407.8 2.7 copy-start.23
  423.6 292.6 %all-reduce.3.cloned.1.call-start = ((), (), s32[]{:S(2)}) async-start(), calls=%async_computation.13 | async-start | bytes 12582912 | tf_op jit(solution)/shard_map/psum | solution.py:199
  423.8 8.2 %copy-start.32 = (bf16[2048,1024]{1,0:T(8,128)(2,1)S(1)}, bf16[2048,1024]{1,0:T(8,128)(2,1)}, u32[]{:S(2)}) copy-start(bf16[2048,1024]{1,0:T(8,128)(2,1)} %all-gather.20.cloned.1.call-done) | copy-start | bytes 12582916
  423.8 8.2 %copy-start.38 = (bf16[2048,1024]{1,0:T(8,128)(2,1)S(1)}, bf16[2048,1024]{1,0:T(8,128)(2,1)}, u32[]{:S(2)}) copy-start(bf16[2048,1024]{1,0:T(8,128)(2,1)} %copy-done.37) | copy-start | bytes 12582916
  439.3 55.9 %copy-start.15 = (bf16[16,64,512]{2,1,0:T(8,128)(2,1)S(1)}, bf16[16,64,512]{2,1,0:T(8,128)(2,1)}, u32[]{:S(2)}) copy-start(bf16[16,64,512]{2,1,0:T(8,128)(2,1)} %copy-done.14) | copy-start | bytes 3145732
  495.2 3.1 copy-start.18
  495.2 3.1 copy-start.34
  498.3 1.6 copy-start.9
  498.3 1.8 copy-start.24
  498.3 2.5 copy-start.35
  500.8 2.8 copy-start.27
  716.2 6.8 copy-start.10
Sparse Core Ops, SparseCore 0:
  9.6 25.2 all-gather.9
  36.5 22.5 all-gather.13
  60.6 22.5 all-gather.15
  84.6 22.5 all-gather.11
  108.6 22.5 all-gather.17
  137.6 34.4 all-gather.19
  206.0 44.5 reduce-scatter.3
  259.3 34.4 all-gather.21
  315.2 44.5 reduce-scatter.5
  423.7 71.3 reduce-scatter.7
  499.6 216.4 all-reduce.2

commit v2 on v1

--- a/solution.py
+++ b/solution.py
@@ -1,10 +1,15 @@
+import functools
+
 import jax
 import jax.numpy as jnp
 from jax import lax
+from jax.experimental import pallas as pl
+from jax.experimental.pallas import tpu as pltpu
 from jax.sharding import PartitionSpec as P
 
 HEAD_DIM = 64
 BLOCK = 25
+MESH = pl.DeviceIdType.MESH
 
 
 norm_eps = 1e-05
@@ -19,6 +24,305 @@
 
 def exact_gelu(values):
     return jax.nn.gelu(values, approximate=False)
+
+
+def _gather_kernel(sizes, *refs):
+    n = len(sizes)
+    ins, outs = refs[:n], refs[n : 2 * n]
+    own_sem, c_send, c_recv, y_send, y_recv, x_send, x_recv, f_send, f_recv, g_send, g_recv = refs[2 * n :]
+    dp, me = lax.axis_index("dp"), lax.axis_index("seq")
+    half = lax.rem(dp, 2)
+    core, across, side = (dp, me ^ 1), (dp, me ^ 2), (dp ^ 1, me)
+    barrier = pltpu.get_barrier_semaphore()
+    for peer in (core, across, side):
+        pl.semaphore_signal(barrier, inc=1, device_id=peer, device_id_type=MESH)
+    pl.semaphore_wait(barrier, 3)
+
+    def remote(src, dst, send, recv, peer):
+        return pltpu.make_async_remote_copy(
+            src_ref=src, dst_ref=dst, send_sem=send, recv_sem=recv, device_id=peer, device_id_type=MESH
+        )
+
+    chunks = []
+    for a, rows in enumerate(sizes):
+        step = min(rows // 2, 256)
+        chunks += [(a, rows, off, step) for off in range(0, rows // 2, step)]
+
+    def region(ref, rows, shard, part, off, step):
+        start = pl.multiple_of(shard * rows + part * (rows // 2) + off, 16)
+        return ref.at[pl.ds(start, step), :]
+
+    waits = []
+    crossing = []
+    for j, (a, rows, off, step) in enumerate(chunks):
+        src = region(ins[a], rows, 0, half, off, step)
+        copy = remote(src, region(outs[a], rows, me, half, off, step), y_send.at[j], y_recv.at[j], across)
+        copy.start()
+        crossing.append(copy)
+    core_copies = []
+    for a, rows in enumerate(sizes):
+        home = outs[a].at[pl.ds(pl.multiple_of(me * rows, 16), rows), :]
+        copy = remote(ins[a], home, c_send.at[a], c_recv.at[a], core)
+        copy.start()
+        core_copies.append(copy)
+        keep = pltpu.make_async_copy(ins[a], home, own_sem.at[a])
+        keep.start()
+        waits.append(keep)
+    sides, firsts, seconds = [], [], []
+    for j in range(len(chunks) + 1):
+        if j < len(chunks):
+            a, rows, off, step = chunks[j]
+            crossing[j].wait_recv()
+            got = region(outs[a], rows, me ^ 2, half, off, step)
+            copy = remote(got, got, x_send.at[j], x_recv.at[j], side)
+            copy.start()
+            sides.append(copy)
+            copy = remote(got, got, f_send.at[j], f_recv.at[j], core)
+            copy.start()
+            firsts.append(copy)
+        if j >= 1:
+            a, rows, off, step = chunks[j - 1]
+            sides[j - 1].wait_recv()
+            got = region(outs[a], rows, me ^ 2, 1 - half, off, step)
+            copy = remote(got, got, g_send.at[j - 1], g_recv.at[j - 1], core)
+            copy.start()
+            seconds.append(copy)
+    for copy in waits:
+        copy.wait()
+    for copy in crossing + sides:
+        copy.wait_send()
+    for copy in core_copies + firsts + seconds:
+        copy.wait()
+
+
+def gather_weights(arrays):
+    sizes = tuple(a.shape[0] for a in arrays)
+    n = len(arrays)
+    m = sum(max(1, r // 512) for r in sizes)
+    dma = pltpu.SemaphoreType.DMA
+    return pl.pallas_call(
+        functools.partial(_gather_kernel, sizes),
+        out_shape=[jax.ShapeDtypeStruct((4 * a.shape[0], a.shape[1]), a.dtype) for a in arrays],
+        in_specs=[pl.BlockSpec(memory_space=pltpu.VMEM)] * n,
+        out_specs=[pl.BlockSpec(memory_space=pl.ANY)] * n,
+        scratch_shapes=[dma((n,))] * 3 + [dma((m,))] * 8,
+        compiler_params=pltpu.CompilerParams(
+            collective_id=0, has_side_effects=True, vmem_limit_bytes=32 << 20
+        ),
+        name="gather_weights",
+    )(*arrays)
+
+
+def _row_loop(rows, step, body):
+    def run(i, carry):
+        body(pl.ds(pl.multiple_of(i * step, step), step))
+        return carry
+
+    lax.fori_loop(0, rows // step, run, 0)
+
+
+def _reduce_kernel(dp_n, slab, terms, vec, rec, out, vec_out, rec_out, *scr):
+    (own, core_in, y_in, x_in, z_in, res, v_core, v_y, v_x, v_z, v_sum) = scr[:11]
+    (load_sem, c_s, c_r, y_s, y_r, x_s, x_r, z_s, z_r, zg_s, zg_r, xg_s, xg_r, out_sem, vs, vr, ws, wr) = scr[11:]
+    f32, bf16 = jnp.float32, jnp.bfloat16
+    count = out.shape[0] // slab
+    nz = dp_n // 2
+    dp, me = lax.axis_index("dp"), lax.axis_index("seq")
+    x, z, y, c = lax.rem(dp, 2), lax.div(dp, 2), lax.div(me, 2), lax.rem(me, 2)
+    core, across, side = (dp, me ^ 1), (dp, me ^ 2), (dp ^ 1, me)
+    others = [(lax.rem(z + o, nz) * 2 + x, me) for o in range(1, nz)]
+    barrier = pltpu.get_barrier_semaphore()
+    for peer in [core, across, side] + others:
+        pl.semaphore_signal(barrier, inc=1, device_id=peer, device_id_type=MESH)
+    pl.semaphore_wait(barrier, 3 + len(others))
+
+    def remote(src, dst, send, recv, peer):
+        copy = pltpu.make_async_remote_copy(
+            src_ref=src, dst_ref=dst, send_sem=send, recv_sem=recv, device_id=peer, device_id_type=MESH
+        )
+        copy.start()
+        return copy
+
+    hs = slab // 2
+    ps = hs // nz
+    rs = min(ps, 32)
+    loads, core_c, y_c, x_c, z_c, zg_c, xg_c, outs = [], [], [], [], [], [], [], []
+
+    for k in range(count):
+        rows = pl.ds(k * slab, slab)
+        core_c.append(remote(terms.at[:, 1 - c, rows, :], core_in.at[k], c_s.at[k], c_r.at[k], core))
+        load = pltpu.make_async_copy(terms.at[:, c, rows, :], own.at[k], load_sem.at[k])
+        load.start()
+        loads.append(load)
+
+    small = [remote(vec, v_core, vs.at[0], vr.at[0], core)]
+    rec_out[dp, me] = rec[...]
+    small_rec = [remote(rec_out.at[dp, me], rec_out.at[dp, me], ws.at[0], wr.at[0], core)]
+
+    def stage_core(k):
+        loads[k].wait()
+        core_c[k].wait_recv()
+
+        def add(r):
+            for p in range(2):
+                own[k, p, r] = (own[k, p, r].astype(f32) + core_in[k, p, r].astype(f32)).astype(bf16)
+
+        _row_loop(slab, 16, add)
+        y_c.append(remote(own.at[k, 1 - y], y_in.at[k], y_s.at[k], y_r.at[k], across))
+
+    def stage_y(k):
+        y_c[k].wait_recv()
+
+        def add(r):
+            own[k, y, r] = (own[k, y, r].astype(f32) + y_in[k, r].astype(f32)).astype(bf16)
+
+        _row_loop(slab, 32, add)
+        give = pl.ds(pl.multiple_of((1 - x) * hs, 16), hs)
+        x_c.append(remote(own.at[k, y, give], x_in.at[k], x_s.at[k], x_r.at[k], side))
+
+    def stage_x(k):
+        x_c[k].wait_recv()
+
+        def add(r):
+            at = pl.ds(pl.multiple_of(x * hs + r.start, 16), r.size)
+            own[k, y, at] = (own[k, y, at].astype(f32) + x_in[k, r].astype(f32)).astype(bf16)
+
+        _row_loop(hs, rs, add)
+        copies = []
+        for o in range(1, nz):
+            piece = pl.ds(pl.multiple_of(x * hs + lax.rem(z + o, nz) * ps, 16), ps)
+            copies.append(
+                remote(own.at[k, y, piece], z_in.at[k, o], z_s.at[k, o], z_r.at[k, o], others[o - 1])
+            )
+        z_c.append(copies)
+
+    def stage_z(k):
+        for copy in z_c[k]:
+            copy.wait_recv()
+
+        def add(r):
+            at = pl.ds(pl.multiple_of(x * hs + z * ps + r.start, 16), r.size)
+            total = own[k, y, at].astype(f32)
+            for o in range(1, nz):
+                total += z_in[k, o, r].astype(f32)
+            res[k, at] = total.astype(bf16)
+
+        _row_loop(ps, rs, add)
+        mine = res.at[k, pl.ds(pl.multiple_of(x * hs + z * ps, 16), ps)]
+        zg_c.append(
+            [remote(mine, mine, zg_s.at[k, o], zg_r.at[k, o], others[o - 1]) for o in range(1, nz)]
+        )
+
+    def stage_zg(k):
+        for copy in zg_c[k]:
+            copy.wait_recv()
+        mine = res.at[k, pl.ds(pl.multiple_of(x * hs, 16), hs)]
+        xg_c.append(remote(mine, mine, xg_s.at[k], xg_r.at[k], side))
+
+    def stage_xg(k):
+        xg_c[k].wait_recv()
+        copy = pltpu.make_async_copy(res.at[k], out.at[pl.ds(k * slab, slab), :], out_sem.at[k])
+        copy.start()
+        outs.append(copy)
+
+    def small_stage(t):
+        if t == 0:
+            small[0].wait_recv()
+            v_sum[0] = vec[...] + v_core[...]
+            small.append(remote(v_sum.at[0], v_y, vs.at[1], vr.at[1], across))
+            small_rec[0].wait_recv()
+            pair = rec_out.at[dp, pl.ds(y * 2, 2)]
+            small_rec.append(remote(pair, pair, ws.at[1], wr.at[1], across))
+        elif t == 1:
+            small[1].wait_recv()
+            v_sum[1] = v_sum[0] + v_y[...]
+            small.append(remote(v_sum.at[1], v_x, vs.at[2], vr.at[2], side))
+            small_rec[1].wait_recv()
+            quad = rec_out.at[dp]
+            small_rec.append(remote(quad, quad, ws.at[2], wr.at[2], side))
+        elif t == 2:
+            small[2].wait_recv()
+            v_sum[2] = v_sum[1] + v_x[...]
+            small_rec[2].wait_recv()
+            pair = rec_out.at[pl.ds(z * 2, 2)]
+            for o in range(1, nz):
+                small.append(remote(v_sum.at[2], v_z.at[o], vs.at[2 + o], vr.at[2 + o], others[o - 1]))
+                small_rec.append(remote(pair, pair, ws.at[2 + o], wr.at[2 + o], others[o - 1]))
+        elif t == 3:
+            total = v_sum[2]
+            for o in range(1, nz):
+                small[2 + o].wait_recv()
+                small_rec[2 + o].wait_recv()
+                total = total + v_z[o]
+            vec_out[...] = total
+
+    stages = [stage_y, stage_x, stage_z, stage_zg, stage_xg]
+    started = 0
+    for t in range(max(count, 4) + len(stages)):
+        for _ in range(2):
+            if started < count:
+                stage_core(started)
+                started += 1
+        for d, stage in enumerate(stages):
+            if 0 <= t - d < count:
+                stage(t - d)
+        small_stage(t)
+    for copy in core_c + y_c + x_c + xg_c + small + small_rec:
+        copy.wait_send()
+    for copies in z_c + zg_c:
+        for copy in copies:
+            copy.wait_send()
+    for copy in outs:
+        copy.wait()
+
+
+def reduce_gradients(dp_n, terms, vec, rec):
+    rows, width = terms.shape[2:]
+    slab = max(256, 16 * dp_n)
+    count, nz = rows // slab, dp_n // 2
+    items = rec.shape[0]
+    bf16, f32 = jnp.bfloat16, jnp.float32
+    dma, vmem = pltpu.SemaphoreType.DMA, pltpu.VMEM
+    v_shape = vec.shape
+    return pl.pallas_call(
+        functools.partial(_reduce_kernel, dp_n, slab),
+        out_shape=[
+            jax.ShapeDtypeStruct((rows, width), bf16),
+            jax.ShapeDtypeStruct(v_shape, f32),
+            jax.ShapeDtypeStruct((dp_n, 4) + rec.shape, f32),
+        ],
+        in_specs=[
+            pl.BlockSpec(memory_space=pl.ANY),
+            pl.BlockSpec(memory_space=pltpu.VMEM),
+            pl.BlockSpec(memory_space=pltpu.VMEM),
+        ],
+        out_specs=[
+            pl.BlockSpec(memory_space=pl.ANY),
+            pl.BlockSpec(memory_space=pltpu.VMEM),
+            pl.BlockSpec(memory_space=pltpu.VMEM),
+        ],
+        scratch_shapes=[
+            vmem((count, 2, slab, width), bf16),
+            vmem((count, 2, slab, width), bf16),
+            vmem((count, slab, width), bf16),
+            vmem((count, slab // 2, width), bf16),
+            vmem((count, nz, slab // 2 // nz, width), bf16),
+            vmem((count, slab, width), bf16),
+            vmem(v_shape, f32),
+            vmem(v_shape, f32),
+            vmem(v_shape, f32),
+            vmem((nz,) + v_shape, f32),
+            vmem((3,) + v_shape, f32),
+        ]
+        + [dma((count,))] * 7
+        + [dma((count, nz))] * 4
+        + [dma((count,))] * 3
+        + [dma((2 + nz,))] * 4,
+        compiler_params=pltpu.CompilerParams(
+            collective_id=1, has_side_effects=True, vmem_limit_bytes=60 << 20
+        ),
+        name="reduce_gradients",
+    )(terms, vec, rec)
 
 
 def split_heads(rows):
@@ -78,6 +382,7 @@
 
 
 def local(
+    dp_n,
     tokens,
     time_embed,
     lengths,
@@ -111,18 +416,8 @@
     def mm(a, b, dims):
         return lax.dot_general(a, b, (dims, ((), ())), preferred_element_type=f32)
 
-    def gather(a):
-        return lax.all_gather(a, "seq", axis=0, tiled=True)
-
-    def scatter_sum(a):
-        return lax.psum_scatter(a, "seq", scatter_dimension=0, tiled=True)
-
-    full_time, full_query, full_key, full_value, full_out = (
-        gather(w_time),
-        gather(w_query),
-        gather(w_key),
-        gather(w_value),
-        gather(w_out),
+    full_time, full_query, full_key, full_value, full_out, full_in, full_down = gather_weights(
+        [w_time, w_query, w_key, w_value, w_out, w_in, w_down]
     )
     own_lengths = lax.dynamic_slice_in_dim(lengths, seq_rank * item_count, item_count, 0)
     slot_index = lax.broadcasted_iota(jnp.int32, (item_count, slot_count), 1)
@@ -147,27 +442,22 @@
     first_norm, first_pull = jax.vjp(
         layer_norm, resid + attn_out, gain_one.astype(f32), shift_one.astype(f32)
     )
-    first_group = gather(first_norm.astype(bf16))
-    bias_in = lax.dynamic_slice_in_dim(b_in, seq_rank * w_in.shape[0], w_in.shape[0], 0)
-    hidden_pre = mm(first_group, w_in, ((1,), (1,))) + bias_in.astype(f32)
+    first_low = first_norm.astype(bf16)
+    hidden_pre = mm(first_low, full_in, ((1,), (1,))) + b_in.astype(f32)
     hidden, gelu_pull = jax.vjp(exact_gelu, hidden_pre)
     hidden_low = hidden.astype(bf16)
-    ffn_part = mm(hidden_low, w_down, ((1,), (0,))).astype(bf16)
-    ffn_out = scatter_sum(ffn_part).astype(f32) + b_down.astype(f32)
+    ffn_out = mm(hidden_low, full_down, ((1,), (0,))) + b_down.astype(f32)
     second_norm, second_pull = jax.vjp(
         layer_norm, first_norm + ffn_out, gain_two.astype(f32), shift_two.astype(f32)
     )
     layer_out = (second_norm * row_keep).astype(bf16)
     grad_second_in, grad_gain_two, grad_shift_two = second_pull(cotangent.astype(f32) * row_keep)
     grad_ffn = grad_second_in.astype(bf16)
-    grad_group = gather(grad_ffn)
-    grad_hidden = mm(grad_group, w_down, ((1,), (1,)))
+    grad_hidden = mm(grad_ffn, full_down, ((1,), (1,)))
     grad_pre = gelu_pull(grad_hidden)[0].astype(bf16)
-    back_part = mm(grad_pre, w_in, ((1,), (0,))).astype(bf16)
-    grad_first = grad_second_in + scatter_sum(back_part).astype(f32)
-    term_in = mm(grad_pre, first_group, ((0,), (0,))).astype(bf16)
-    term_down = mm(hidden_low, grad_group, ((0,), (0,))).astype(bf16)
-    sum_ffn = lax.psum(jnp.concatenate([term_in, term_down], axis=0), "dp").astype(f32)
+    grad_first = grad_second_in + mm(grad_pre, full_in, ((1,), (0,)))
+    term_in = mm(grad_pre, first_low, ((0,), (0,))).astype(bf16)
+    term_down = mm(hidden_low, grad_ffn, ((0,), (0,))).astype(bf16)
     grad_first_in, grad_gain_one, grad_shift_one = first_pull(grad_first)
     grad_attn = grad_first_in.astype(bf16)
     grad_mixed = mm(grad_attn, full_out, ((1,), (1,))).astype(bf16)
@@ -187,56 +477,48 @@
     )
     grad_tokens = grad_resid.astype(bf16)
     grad_time = jnp.sum(grad_resid.reshape(item_count, slot_count, width), axis=1).astype(bf16)
-    terms = [
-        mm(resid_low, grad_query, ((0,), (0,))),
-        mm(resid_low, grad_key, ((0,), (0,))),
-        mm(resid_low, grad_value, ((0,), (0,))),
-        mm(mixed_rows, grad_attn, ((0,), (0,))),
+    parts = [
+        mm(resid_low, grad_query, ((0,), (0,))).astype(bf16),
+        mm(resid_low, grad_key, ((0,), (0,))).astype(bf16),
+        mm(resid_low, grad_value, ((0,), (0,))).astype(bf16),
+        mm(mixed_rows, grad_attn, ((0,), (0,))).astype(bf16),
+        term_in,
+        term_down,
     ]
-    group = w_out.shape[0]
-    stacked = jnp.stack([t.astype(bf16).reshape(-1, group, width) for t in terms], axis=1)
-    share = scatter_sum(stacked.reshape(-1, width))
-    sum_attn = lax.psum(share, "dp").astype(f32)
-    small = jnp.concatenate(
+    terms = jnp.concatenate([t.reshape(2, 2, -1, width) for t in parts], axis=2)
+    vec = jnp.stack(
         [
-            jnp.stack(
-                [
-                    jnp.sum(grad_query, axis=0, dtype=f32),
-                    jnp.sum(grad_value, axis=0, dtype=f32),
-                    jnp.sum(grad_attn, axis=0, dtype=f32),
-                    jnp.sum(grad_ffn, axis=0, dtype=f32),
-                    grad_gain_one,
-                    grad_shift_one,
-                    grad_gain_two,
-                    grad_shift_two,
-                ]
-            ).astype(bf16),
-            jnp.sum(grad_pre, axis=0, dtype=f32).reshape(-1, width).astype(bf16),
-            time_embed,
-            grad_time,
-        ],
-        axis=0,
-    )
-    every = lax.all_gather(small, ("dp", "seq"), axis=0)
-    vectors = jnp.sum(every[:, :8], axis=0, dtype=f32)
-    hidden_rows = every.shape[1] - 8 - 2 * item_count
-    in_parts = every[:, 8 : 8 + hidden_rows].reshape(-1, b_in.shape[0])
-    grad_b_in = jnp.sum(in_parts, axis=0, dtype=f32)
-    time_rows = every[:, 8 + hidden_rows : 8 + hidden_rows + item_count].reshape(-1, width)
-    time_grads = every[:, 8 + hidden_rows + item_count :].reshape(-1, width)
+            jnp.sum(grad_query, axis=0, dtype=f32),
+            jnp.sum(grad_value, axis=0, dtype=f32),
+            jnp.sum(grad_attn, axis=0, dtype=f32),
+            jnp.sum(grad_ffn, axis=0, dtype=f32),
+            grad_gain_one,
+            grad_shift_one,
+            grad_gain_two,
+            grad_shift_two,
+        ]
+    )
+    vec = jnp.concatenate([vec, jnp.sum(grad_pre, axis=0, dtype=f32).reshape(-1, width)], axis=0)
+    vec = jnp.pad(vec, ((0, -vec.shape[0] % 8), (0, 0)))
+    rec = jnp.stack([time_embed, grad_time], axis=1).astype(f32).reshape(item_count, -1, 128)
+    sums, vectors, every = reduce_gradients(dp_n, terms, vec, rec)
+    every = every.reshape(-1, 2, width)
+    time_rows, time_grads = every[:, 0].astype(bf16), every[:, 1].astype(bf16)
     own_columns = lax.dynamic_slice_in_dim(time_rows, seq_rank * rows, rows, 1)
     grad_w_time = mm(own_columns, time_grads, ((0,), (0,)))
     grad_b_time = jnp.sum(time_grads, axis=0, dtype=f32)
+    grad_b_in = vectors[8 : 8 + b_in.shape[0] // width].reshape(-1)
+    sums = sums.astype(f32)
+    ends = [0]
+    for t in parts:
+        ends.append(ends[-1] + t.shape[0] // 4)
+    shares = [sums[lo:hi] for lo, hi in zip(ends[:-1], ends[1:])]
     return (
         layer_out,
         grad_tokens,
-        sum_attn[:group],
-        sum_attn[group : 2 * group],
-        sum_attn[2 * group : 3 * group],
-        sum_attn[3 * group :],
+        *shares[:4],
         grad_w_time,
-        sum_ffn[: w_in.shape[0]],
-        sum_ffn[w_in.shape[0] :],
+        *shares[4:],
         vectors[0],
         vectors[1],
         vectors[2],
@@ -295,4 +577,4 @@
         P(),
         P(),
     )
-    return jax.shard_map(local, mesh=mesh, in_specs=in_specs, out_specs=out_specs, check_vma=False)
+    return jax.shard_map(functools.partial(local, mesh.shape["dp"]), mesh=mesh, in_specs=in_specs, out_specs=out_specs, check_vma=False)

time: 741 us -> 544 us (0.73)
  waiting for transfers between devices: 443 us -> 0 us
  Pallas kernels: 0 us -> 291 us
  blocking collectives: 51.7 us -> 0 us
  local copies, waits for them, and re-layouts: 35.2 us -> 55.9 us
  between operations: 15.6 us -> 2.3 us
  matrix products: 138 us -> 151 us
  other arithmetic: 47.2 us -> 35.1 us
    pallas_call x0 -> x2, Pallas kernels: none -> 291 us  [the longest x1 198 us: reduce_gradients(): pl.pallas_call(functools.partial(_reduce_kernel, dp_n, slab), out_shape=[...]
    psum x1 -> x0, waiting for transfers between devices: 157 us -> none  [local(): sum_attn = lax.psum(share, 'dp').astype(f32)]
    reduce_scatter x3 -> x0, waiting for transfers between devices: 145 us -> none  [scatter_sum(): return lax.psum_scatter(a, 'seq', scatter_dimension=0, tiled=True)]
    all_gather x7 -> x0, waiting for transfers between devices: 138 us -> none  [gather(): return lax.all_gather(a, 'seq', axis=0, tiled=True)]
    all_gather x1 -> x0, blocking collectives: 51.7 us -> none  [local(): every = lax.all_gather(small, ('dp', 'seq'), axis=0)]
    unnamed x78 -> x95, local copies, waits for them, and re-layouts: 9.91 us -> 29.1 us
    dot_general x20, matrix products: 96.6 us -> 109 us  [mm(): return lax.dot_general(a, b, (dims, ((), ())), preferred_element_type=f32)]
    another operation x1, local copies, waits for them, and re-layouts: 7.95 us -> 0.04 us  [local(): jnp.stack([t.astype(bf16).reshape(-1, group, width) for t in terms], axis=1)]
  transfers between devices with their start and end apart: 11 -> 0, of which waited for: 11 -> 0; matrix products, arithmetic and copies ran while one was open for 10% -> 0% of each run, Pallas kernels for 0% -> 0%
where the time goes in v2:
time: 544 us; the launch traced here: 535 us
  Pallas kernels  291 us (53%)
  matrix products  151 us (28%)
  local copies, waits for them, and re-layouts  55.9 us (10%)
  other arithmetic  35.1 us (6%)
    pallas_call x1, Pallas kernels, reduce_gradients(): pl.pallas_call(functools.partial(_reduce_kernel, dp_n, slab), out_shape=[...  198 us
    dot_general x20, matrix products, mm(): return lax.dot_general(a, b, (dims, ((), ())), preferred_element_type=f32)  109 us
    pallas_call x1, Pallas kernels, gather_weights(): pl.pallas_call(functools.partial(_gather_kernel, sizes), out_shape=[jax.S...  93.5 us
    unnamed x95, local copies, waits for them, and re-layouts  29.1 us
    convert_element_type x1, other arithmetic, attend_backward(): scores_low = grad_scores.astype(jnp.bfloat16)  11.8 us
    dot_general x1, matrix products, attend_backward(): jnp.einsum('qhd,khd->hqk', grad_heads, split_heads(values), preferred_ele...  11.1 us

profile of v2, /device:TPU:0, one launch (start us, length us, event | category | flops | bytes accessed | tf_op | source)
XLA Modules:
  0.0 535.1 jit_solution(12369567429363027868)
XLA Ops:
  0.7 1.2 dynamic_slice.8
  2.6 0.7 convert_element_type.232
  3.3 0.7 convert_element_type.233
  3.9 0.7 convert_element_type.238
  4.6 0.7 convert_element_type.224
  8.1 0.7 convert_element_type.235
  8.8 1.6 copy-done
  10.3 1.6 copy-done.1
  11.9 1.0 copy-done.2
  13.0 1.0 copy-done.3
  14.0 1.0 copy-done.4
  15.1 1.0 copy-done.5
  16.1 1.0 copy-done.6
  17.1 93.5 %gather_weights.1 = (bf16[1024,1024]{1,0:T(8,128)(2,1)S(1)}, bf16[1024,1024]{1,0:T(8,128)(2,1)S(1)}, bf16[1024,1024]{1,0:T(8,128)(2,1)S(1)}, bf16[1024,1024]{1,0...) custom-call(bf16[256,1024]{1,0:T(8,128)(2,1)S(1)} %copy-done.2, ...), custom_call_target="tpu_custom_call" | custom-call | tf_op jit(solution)/shard_map/gather_weights/pallas_call | solution.py:103
  110.7 1.4 copy-done.10
  112.4 0.9 copy-done.7
  114.0 1.3 add_convert_fusion.1
  115.2 1.3 copy.53
  116.5 3.2 add_convert_fusion.2
  119.7 1.3 copy.52
  121.0 4.1 convolution_convert_fusion.7
  125.2 1.5 copy.54
  126.7 9.1 %fusion.43 = (f32[16,512]{1,0:T(8,128)S(1)}, f32[16,512,512]{1,2,0:T(8,128)}) fusion(bf16[512,16,64]{0,2,1:T(8,128)(2,1)} %bitcast.102, bf16[512,16,64]{0,2,1:T(8,128)(2,1)S(1)} %bitcast.98, pred[512]{0:T(512)(128)(4,1)S(1)} %get-tuple-element.91), kind=kOutput, calls=%fused_computation.107 | convolution fusion | flops 549445632 | bytes 18907648 | tf_op jit(solution)/shard_map/qhd,khd->hqk/dot_general | solution.py:333
  135.9 8.4 %fusion = f32[16,512]{1,0:T(8,128)S(1)} fusion(f32[16,512,512]{1,2,0:T(8,128)} %get-tuple-element.77, f32[16,512]{1,0:T(8,128)S(1)} %get-tuple-element.76), kind=kLoop, calls=%fused_computation.6 | loop fusion | flops 8380416 | bytes 16842752 | tf_op jit(solution)/shard_map/reduce_sum | solution.py:343
  144.3 7.8 %fusion.16 = bf16[16,64,512]{2,1,0:T(8,128)(2,1)S(1)} fusion(bf16[512,16,64]{0,2,1:T(8,128)(2,1)S(1)} %bitcast.106, f32[16,512,512]{1,2,0:T(8,128)} %get-tuple-element.77, f32[16,512]{1,0:T(8,128)S(1)} %fusion, f32[16,512]{1,0:T(8,128)S(1)} %get-tuple-element.76), kind=kOutput, calls=%fused_computation.65 | convolution fusion | flops 549978112 | bytes 18939904 | tf_op jit(solution)/shard_map/hqk,khd->qhd/dot_general | solution.py:345
  152.1 1.4 fusion.44
  153.9 28.4 %multiply_convert_fusion.1 = (bf16[512,4096]{1,0:T(8,128)(2,1)S(1)}, f32[512,4096]{1,0:T(8,128)}, f32[512,4096]{1,0:T(8,128)}) fusion(f32[4096]{0:T(1024)S(1)} %convert_element_type.235, bf16[4096,1024]{1,0:T(8,128)(2,1)} %get-tuple-element.34, f32[512,1024]{1,0:T(8,128)S(1)} %get-tuple-element.79, f32[1024]{0:T(1024)S(1)} %convert_element_type.233, ...), kind=kOutput, calls=%fused_computation.14 | convolution fusion | flops 4436000768 | bytes 31485952 | tf_op jit(solution)/shard_map/dot_general | solution.py:417
  182.4 4.8 fusion.45
  187.5 1.0 multiply_reduce_fusion.1
  188.5 2.0 fusion.36
  190.8 13.9 %convert_reduce_fusion = (f32[4096]{0:T(1024)S(1)}, bf16[512,4096]{1,0:T(8,128)(2,1)S(1)}) fusion(f32[512,4096]{1,0:T(8,128)} %get-tuple-element.56, f32[512,4096]{1,0:T(8,128)} %get-tuple-element.80, f32[4096]{0:T(1024)S(1)} %convert_element_type.235, bf16[512,1024]{1,0:T(8,128)(2,1)S(1)} %get-tuple-element.48, bf16[4096,1024]{1,0:T(8,128)(2,1)} %get-tuple-element.35), kind=kOutput, calls=%fused_computation.11 | convolution fusion | flops 4330614784 | bytes 30441472 | tf_op jit(solution)/shard_map/dot_general | solution.py:417
  204.8 11.2 %multiply_reduce_fusion.2 = (f32[1024]{0:T(1024)S(1)}, f32[512]{0:T(512)S(1)}, f32[1024]{0:T(1024)S(1)}, f32[512,1024]{1,0:T(8,128)}) fusion(f32[512,1024]{1,0:T(8,128)S(1)} %get-tuple-element.79, f32[512]{0:T(512)S(1)} %fusion.29, f32[512]{0:T(512)S(1)} %broadcast_multiply_fusion.1, f32[1024]{0:T(1024)S(1)} %convert_element_type.232, ...), kind=kOutput, calls=%fused_computation.34 | convolution fusion | flops 4300207616 | bytes 18894848 | tf_op jit(solution)/shard_map/dot_general | solution.py:417
  216.0 2.9 fusion.35
  219.2 2.3 convolution_convert_fusion.6
  221.5 1.5 copy.56
  223.0 4.1 convolution_convert_fusion.2
  227.1 9.6 %convert_reduce_fusion.3 = (f32[16,64]{1,0:T(8,128)S(1)}, bf16[16,64,512]{2,1,0:T(8,128)(2,1)}) fusion(bf16[512,16,64]{0,2,1:T(8,128)(2,1)S(1)} %bitcast.100, f32[16,512,512]{1,2,0:T(8,128)} %get-tuple-element.77, f32[16,512]{1,0:T(8,128)S(1)} %log_add_fusion), kind=kOutput, calls=%fused_computation.37 | convolution fusion | flops 546831360 | bytes 18911232 | tf_op jit(solution)/shard_map/hqk,qhd->khd/dot_general | solution.py:356
  236.8 9.6 %convolution_convert_fusion.1 = bf16[4096,1024]{1,0:T(8,128)(2,1)} fusion(bf16[512,4096]{1,0:T(8,128)(2,1)} %copy-done.41, f32[512,1024]{1,0:T(8,128)S(1)} %copy-done.14, f32[1024]{0:T(1024)S(1)} %convert_element_type.233, f32[1024]{0:T(1024)S(1)} %convert_element_type.232, f32[512]{0:T(512)S(1)} %fusion.29, f32[512]{0:T(512)S(1)} %broadcast_multiply_fusion.1), kind=kOutput, calls=%fused_computation.30 | convolution fusion | flops 4301783040 | bytes 14692352 | tf_op jit(solution)/shard_map/dot_general | solution.py:417
  246.4 2.6 convolution_convert_fusion.3
  249.4 6.8 %convolution_convert_fusion = bf16[4096,1024]{1,0:T(8,128)(2,1)} fusion(bf16[512,4096]{1,0:T(8,128)(2,1)S(1)} %copy-done.40, bf16[512,1024]{1,0:T(8,128)(2,1)S(1)} %copy-done.29), kind=kOutput, calls=%fused_computation.29 | convolution fusion | flops 4299161600 | bytes 13631488 | tf_op jit(solution)/shard_map/dot_general | solution.py:417
  256.1 11.1 %multiply_reduce_fusion = (f32[16,512]{1,0:T(8,128)S(1)}, f32[16,512,512]{1,2,0:T(8,128)}) fusion(f32[16,512,512]{1,2,0:T(8,128)} %get-tuple-element.77, f32[16,512]{1,0:T(8,128)S(1)} %log_add_fusion, bf16[512,16,64]{0,2,1:T(8,128)(2,1)S(1)} %bitcast.101, bf16[512,16,64]{0,2,1:T(8,128)(2,1)S(1)} %bitcast.107), kind=kOutput, calls=%fused_computation.1 | convolution fusion | flops 549445632 | bytes 35717120 | tf_op jit(solution)/shard_map/qhd,khd->hqk/dot_general | solution.py:359
  267.2 11.8 %multiply_convert_fusion = bf16[16,512,512]{1,2,0:T(8,128)(2,1)S(1)} fusion(f32[16,512,512]{1,2,0:T(8,128)} %get-tuple-element.85, f32[16,512,512]{1,2,0:T(8,128)} %get-tuple-element.77, f32[16,512]{1,0:T(8,128)S(1)} %get-tuple-element.84, f32[16,512]{1,0:T(8,128)S(1)} %log_add_fusion), kind=kLoop, calls=%fused_computation | loop fusion | flops 16777216 | bytes 42008576 | tf_op jit(solution)/shard_map/convert_element_type | solution.py:363
  279.0 2.6 multiply_convert_fusion.2
  281.7 1.5 convert_reduce_fusion.4
  283.6 2.6 fusion.47
  286.4 3.0 fusion.46
  289.5 0.7 copy-done.38
  290.1 2.5 fusion.40
  294.0 2.5 convolution_convert_fusion.5
  296.6 2.8 convolution_convert_fusion.4
  299.4 1.5 constant_dynamic-update-slice_fusion.5
  300.9 1.5 constant_dynamic-update-slice_fusion.4
  302.4 1.5 constant_dynamic-update-slice_fusion.3
  303.9 1.5 constant_dynamic-update-slice_fusion.2
  305.4 7.8 %constant_dynamic-update-slice_fusion.1 = bf16[2,2,3072,1024]{3,2,1,0:T(8,128)(2,1)} fusion(bf16[2,2,3072,1024]{3,2,1,0:T(8,128)(2,1)} %constant_dynamic-update-slice_fusion.2, bf16[2,2,1024,1024]{3,2,1,0:T(8,128)(2,1)} %bitcast.104), kind=kLoop, calls=%fused_computation.77 | loop fusion | bytes 16777216
  313.2 7.9 %constant_dynamic-update-slice_fusion.terms = bf16[2,2,3072,1024]{3,2,1,0:T(8,128)(2,1)} fusion(bf16[2,2,3072,1024]{3,2,1,0:T(8,128)(2,1)} %constant_dynamic-update-slice_fusion.1, bf16[2,2,1024,1024]{3,2,1,0:T(8,128)(2,1)} %bitcast.105), kind=kLoop, calls=%fused_computation.76 | loop fusion | bytes 16777216 | tf_op jit(solution)/shard_map/concatenate | solution.py:488
  321.1 197.7 %reduce_gradients.1 = (bf16[3072,1024]{1,0:T(8,128)(2,1)}, f32[16,1024]{1,0:T(8,128)}, f32[8,4,1,16,128]{4,3,2,1,0:T(8,128)}) custom-call(bf16[2,2,3072,1024]{3,2,1,0:T(8,128)(2,1)} %constant_dynamic-update-slice_fusion.terms, f32[16,1024]{1,0:T(8,128)} %pad.4.vec, f32[1,16,128]{2,1,0:T(8,128)} %reshape.255.rec), custom_call_target="tpu_custom_call" | custom-call | tf_op jit(solution)/shard_map/reduce_gradients/pallas_call | solution.py:287
  518.9 1.0 convert.6
  519.9 0.8 slice_bitcast_fusion
  520.7 1.8 fusion.42
  524.0 1.3 fusion.26
  525.3 3.9 fusion.39
  529.2 1.0 copy-done.12
  530.2 4.4 fusion.38
  (111 shorter events, 9.0 us)
Async XLA Ops:
  0.7 111.4 %copy-start.35 = (bf16[1,1024]{1,0:T(2,128)(2,1)S(1)}, bf16[1,1024]{1,0:T(2,128)(2,1)}, u32[]{:S(2)}) copy-start(bf16[1,1024]{1,0:T(2,128)(2,1)} %param.22) | copy-start | bytes 6148
  8.8 1.6 copy-start
  10.3 1.6 copy-start.1
  11.9 1.0 copy-start.2
  13.0 1.0 copy-start.3
  14.0 1.0 copy-start.4
  15.1 1.0 copy-start.5
  16.1 1.0 copy-start.6
  17.1 96.2 %copy-start.37 = (bf16[1024]{0:T(1024)(128)(2,1)S(1)}, bf16[1024]{0:T(1024)(128)(2,1)}, u32[]{:S(2)}) copy-start(bf16[1024]{0:T(1024)(128)(2,1)} %param.35) | copy-start | bytes 6148
  17.1 96.8 %copy-start.31 = (bf16[512,1024]{1,0:T(8,128)(2,1)S(1)}, bf16[512,1024]{1,0:T(8,128)(2,1)}, u32[]{:S(2)}) copy-start(bf16[512,1024]{1,0:T(8,128)(2,1)} %param.21) | copy-start | bytes 3145732
  110.6 1.4 copy-start.10
  112.0 1.3 copy-start.7
  112.0 1.9 copy-start.9
  126.7 9.2 %copy-start.15 = (bf16[512,1024]{0,1:T(8,128)(2,1)}, bf16[512,1024]{0,1:T(8,128)(2,1)S(1)}, u32[]{:S(2)}) copy-start(bf16[512,1024]{0,1:T(8,128)(2,1)S(1)} %copy.54) | copy-start | bytes 3145732
  135.9 8.4 %copy-start.20 = (bf16[512,1024]{0,1:T(8,128)(2,1)S(1)}, bf16[512,1024]{0,1:T(8,128)(2,1)}, u32[]{:S(2)}) copy-start(bf16[512,1024]{0,1:T(8,128)(2,1)} %copy.52) | copy-start | bytes 3145732
  144.2 7.9 %copy-start.32 = (bf16[512,1024]{1,0:T(8,128)(2,1)S(1)}, bf16[512,1024]{1,0:T(8,128)(2,1)}, u32[]{:S(2)}) copy-start(bf16[512,1024]{1,0:T(8,128)(2,1)} %param.21) | copy-start | bytes 3145732
  152.1 1.8 copy-start.34
  152.1 30.2 %slice-start = ((s8[8388608]{0:T(1024)(128)(4,1)}), s8[4194304]{0:T(1024)(128)(4,1)S(1)}, s32[]{:S(2)}) async-start(s8[8388608]{0:T(1024)(128)(4,1)} %bitcast.137), calls=%async_computation | async-start | bytes 8388608
  153.5 51.3 %copy-start.13 = (f32[512,1024]{1,0:T(8,128)}, f32[512,1024]{1,0:T(8,128)S(1)}, u32[]{:S(2)}) copy-start(f32[512,1024]{1,0:T(8,128)S(1)} %get-tuple-element.79) | copy-start | bytes 6291460
  153.9 28.4 %slice-start.1 = ((s8[8388608]{0:T(1024)(128)(4,1)}), s8[4194304]{0:T(1024)(128)(4,1)S(1)}, s32[]{:S(2)}) async-start(s8[8388608]{0:T(1024)(128)(4,1)} %bitcast.137), calls=%async_computation.1 | async-start | bytes 8388608
  182.3 4.8 copy-start.39
  182.4 5.2 copy-start.22
  190.8 14.0 %copy-start.28 = (bf16[512,1024]{1,0:T(8,128)(2,1)}, bf16[512,1024]{1,0:T(8,128)(2,1)S(1)}, u32[]{:S(2)}) copy-start(bf16[512,1024]{1,0:T(8,128)(2,1)S(1)} %get-tuple-element.48) | copy-start | bytes 3145732
  204.8 11.2 %copy-start.41 = (bf16[512,4096]{1,0:T(8,128)(2,1)}, bf16[512,4096]{1,0:T(8,128)(2,1)S(1)}, u32[]{:S(2)}) copy-start(bf16[512,4096]{1,0:T(8,128)(2,1)S(1)} %get-tuple-element.46) | copy-start | bytes 12582916
  218.9 2.6 copy-start.18
  219.2 2.3 copy-start.30
  227.1 9.7 %copy-start.14 = (f32[512,1024]{1,0:T(8,128)S(1)}, f32[512,1024]{1,0:T(8,128)}, u32[]{:S(2)}) copy-start(f32[512,1024]{1,0:T(8,128)} %copy-done.13) | copy-start | bytes 6291460
  236.8 9.6 %copy-start.26 = (bf16[16,64,512]{2,1,0:T(8,128)(2,1)S(1)}, bf16[16,64,512]{2,1,0:T(8,128)(2,1)}, u32[]{:S(2)}) copy-start(bf16[16,64,512]{2,1,0:T(8,128)(2,1)} %get-tuple-element.90) | copy-start | bytes 3145732
  236.8 9.7 %copy-start.33 = (bf16[512,1024]{1,0:T(8,128)(2,1)S(1)}, bf16[512,1024]{1,0:T(8,128)(2,1)}, u32[]{:S(2)}) copy-start(bf16[512,1024]{1,0:T(8,128)(2,1)} %param.21) | copy-start | bytes 3145732
  246.4 2.6 copy-start.29
  246.4 3.0 copy-start.40
  249.4 6.8 %copy-start.21 = (bf16[512,1024]{0,1:T(8,128)(2,1)S(1)}, bf16[512,1024]{0,1:T(8,128)(2,1)}, u32[]{:S(2)}) copy-start(bf16[512,1024]{0,1:T(8,128)(2,1)} %copy.52) | copy-start | bytes 3145732
  267.2 11.8 %copy-start.17 = (bf16[512,1024]{0,1:T(8,128)(2,1)S(1)}, bf16[512,1024]{0,1:T(8,128)(2,1)}, u32[]{:S(2)}) copy-start(bf16[512,1024]{0,1:T(8,128)(2,1)} %copy.53) | copy-start | bytes 3145732
  279.0 2.6 copy-start.16
  281.7 1.5 copy-start.25
  281.7 2.0 copy-start.11
  286.3 3.1 copy-start.8
  286.3 3.1 copy-start.19
  286.3 3.1 copy-start.27
  286.3 3.8 copy-start.38
  290.1 2.6 copy-start.36
  299.4 3.0 copy-start.24
  300.9 3.0 copy-start.23
  525.3 4.9 copy-start.12

commit v3 on v2

--- a/solution.py
+++ b/solution.py
@@ -22,16 +22,21 @@
     return center * spread * gain + shift
 
 
-def exact_gelu(values):
-    return jax.nn.gelu(values, approximate=False)
+def gelu_parts(values):
+    half = 0.5 + 0.5 * lax.erf(values * 0.5**0.5)
+    density = jnp.exp(-0.5 * values * values) * (0.5 / jnp.pi) ** 0.5
+    return values * half, half + values * density
 
 
 def _gather_kernel(sizes, *refs):
     n = len(sizes)
-    ins, outs = refs[:n], refs[n : 2 * n]
-    own_sem, c_send, c_recv, y_send, y_recv, x_send, x_recv, f_send, f_recv, g_send, g_recv = refs[2 * n :]
+    given, outs, ins = refs[:n], refs[n : 2 * n], refs[2 * n : 3 * n]
+    load_sem, own_sem, c_send, c_recv, y_send, y_recv, x_send, x_recv, f_send, f_recv, g_send, g_recv = refs[3 * n :]
     dp, me = lax.axis_index("dp"), lax.axis_index("seq")
     half = lax.rem(dp, 2)
+    loads = [pltpu.make_async_copy(given[a], ins[a], load_sem.at[a]) for a in range(n)]
+    for load in loads:
+        load.start()
     core, across, side = (dp, me ^ 1), (dp, me ^ 2), (dp ^ 1, me)
     barrier = pltpu.get_barrier_semaphore()
     for peer in (core, across, side):
@@ -55,6 +60,8 @@
     waits = []
     crossing = []
     for j, (a, rows, off, step) in enumerate(chunks):
+        if off == 0:
+            loads[a].wait()
         src = region(ins[a], rows, 0, half, off, step)
         copy = remote(src, region(outs[a], rows, me, half, off, step), y_send.at[j], y_recv.at[j], across)
         copy.start()
@@ -103,9 +110,9 @@
     return pl.pallas_call(
         functools.partial(_gather_kernel, sizes),
         out_shape=[jax.ShapeDtypeStruct((4 * a.shape[0], a.shape[1]), a.dtype) for a in arrays],
-        in_specs=[pl.BlockSpec(memory_space=pltpu.VMEM)] * n,
+        in_specs=[pl.BlockSpec(memory_space=pl.ANY)] * n,
         out_specs=[pl.BlockSpec(memory_space=pl.ANY)] * n,
-        scratch_shapes=[dma((n,))] * 3 + [dma((m,))] * 8,
+        scratch_shapes=[pltpu.VMEM(a.shape, a.dtype) for a in arrays] + [dma((n,))] * 4 + [dma((m,))] * 8,
         compiler_params=pltpu.CompilerParams(
             collective_id=0, has_side_effects=True, vmem_limit_bytes=32 << 20
         ),
@@ -121,7 +128,8 @@
     lax.fori_loop(0, rows // step, run, 0)
 
 
-def _reduce_kernel(dp_n, slab, terms, vec, rec, out, vec_out, rec_out, *scr):
+def _reduce_kernel(dp_n, slab, heights, *refs):
+    terms, (vec, rec, out, vec_out, rec_out), scr = refs[: len(heights)], refs[len(heights) : len(heights) + 5], refs[len(heights) + 5 :]
     (own, core_in, y_in, x_in, z_in, res, v_core, v_y, v_x, v_z, v_sum) = scr[:11]
     (load_sem, c_s, c_r, y_s, y_r, x_s, x_r, z_s, z_r, zg_s, zg_r, xg_s, xg_r, out_sem, vs, vr, ws, wr) = scr[11:]
     f32, bf16 = jnp.float32, jnp.bfloat16
@@ -148,20 +156,33 @@
     rs = min(ps, 32)
     loads, core_c, y_c, x_c, z_c, zg_c, xg_c, outs = [], [], [], [], [], [], [], []
 
+    bases = [sum(heights[:i]) for i in range(len(heights))]
+    pieces = [[] for _ in range(count)]
+    for term, base, height in zip(terms, bases, heights):
+        step = min(height, slab)
+        for off in range(0, height, step):
+            pieces[(base + off) // slab].append((term, off, (base + off) % slab, step))
     for k in range(count):
-        rows = pl.ds(k * slab, slab)
-        core_c.append(remote(terms.at[:, 1 - c, rows, :], core_in.at[k], c_s.at[k], c_r.at[k], core))
-        load = pltpu.make_async_copy(terms.at[:, c, rows, :], own.at[k], load_sem.at[k])
-        load.start()
-        loads.append(load)
+        group = [[], []]
+        for i, (term, off, at, step) in enumerate(pieces[k]):
+            rows, place = pl.ds(off, step), pl.ds(at, step)
+            copy = remote(term.at[:, 1 - c, rows, :], core_in.at[k, :, place, :], c_s.at[k, i], c_r.at[k, i], core)
+            load = pltpu.make_async_copy(term.at[:, c, rows, :], own.at[k, :, place, :], load_sem.at[k, i])
+            load.start()
+            group[0].append(copy)
+            group[1].append(load)
+        core_c.append(group[0])
+        loads.append(group[1])
 
     small = [remote(vec, v_core, vs.at[0], vr.at[0], core)]
     rec_out[dp, me] = rec[...]
     small_rec = [remote(rec_out.at[dp, me], rec_out.at[dp, me], ws.at[0], wr.at[0], core)]
 
     def stage_core(k):
-        loads[k].wait()
-        core_c[k].wait_recv()
+        for load in loads[k]:
+            load.wait()
+        for copy in core_c[k]:
+            copy.wait_recv()
 
         def add(r):
             for p in range(2):
@@ -267,9 +288,9 @@
             if 0 <= t - d < count:
                 stage(t - d)
         small_stage(t)
-    for copy in core_c + y_c + x_c + xg_c + small + small_rec:
+    for copy in y_c + x_c + xg_c + small + small_rec:
         copy.wait_send()
-    for copies in z_c + zg_c:
+    for copies in core_c + z_c + zg_c:
         for copy in copies:
             copy.wait_send()
     for copy in outs:
@@ -277,25 +298,24 @@
 
 
 def reduce_gradients(dp_n, terms, vec, rec):
-    rows, width = terms.shape[2:]
+    width = terms[0].shape[-1]
+    heights = tuple(t.shape[2] for t in terms)
+    rows = sum(heights)
     slab = max(256, 16 * dp_n)
     count, nz = rows // slab, dp_n // 2
+    most = max(1, slab // min(heights))
     items = rec.shape[0]
     bf16, f32 = jnp.bfloat16, jnp.float32
     dma, vmem = pltpu.SemaphoreType.DMA, pltpu.VMEM
     v_shape = vec.shape
     return pl.pallas_call(
-        functools.partial(_reduce_kernel, dp_n, slab),
+        functools.partial(_reduce_kernel, dp_n, slab, heights),
         out_shape=[
             jax.ShapeDtypeStruct((rows, width), bf16),
             jax.ShapeDtypeStruct(v_shape, f32),
             jax.ShapeDtypeStruct((dp_n, 4) + rec.shape, f32),
         ],
-        in_specs=[
-            pl.BlockSpec(memory_space=pl.ANY),
-            pl.BlockSpec(memory_space=pltpu.VMEM),
-            pl.BlockSpec(memory_space=pltpu.VMEM),
-        ],
+        in_specs=[pl.BlockSpec(memory_space=pl.ANY)] * len(terms) + [pl.BlockSpec(memory_space=pltpu.VMEM)] * 2,
         out_specs=[
             pl.BlockSpec(memory_space=pl.ANY),
             pl.BlockSpec(memory_space=pltpu.VMEM),
@@ -314,7 +334,8 @@
             vmem((nz,) + v_shape, f32),
             vmem((3,) + v_shape, f32),
         ]
-        + [dma((count,))] * 7
+        + [dma((count, most))] * 3
+        + [dma((count,))] * 4
         + [dma((count, nz))] * 4
         + [dma((count,))] * 3
         + [dma((2 + nz,))] * 4,
@@ -322,7 +343,7 @@
             collective_id=1, has_side_effects=True, vmem_limit_bytes=60 << 20
         ),
         name="reduce_gradients",
-    )(terms, vec, rec)
+    )(*terms, vec, rec)
 
 
 def split_heads(rows):
@@ -444,7 +465,7 @@
     )
     first_low = first_norm.astype(bf16)
     hidden_pre = mm(first_low, full_in, ((1,), (1,))) + b_in.astype(f32)
-    hidden, gelu_pull = jax.vjp(exact_gelu, hidden_pre)
+    hidden, gelu_slope = gelu_parts(hidden_pre)
     hidden_low = hidden.astype(bf16)
     ffn_out = mm(hidden_low, full_down, ((1,), (0,))) + b_down.astype(f32)
     second_norm, second_pull = jax.vjp(
@@ -454,7 +475,7 @@
     grad_second_in, grad_gain_two, grad_shift_two = second_pull(cotangent.astype(f32) * row_keep)
     grad_ffn = grad_second_in.astype(bf16)
     grad_hidden = mm(grad_ffn, full_down, ((1,), (1,)))
-    grad_pre = gelu_pull(grad_hidden)[0].astype(bf16)
+    grad_pre = (grad_hidden * gelu_slope).astype(bf16)
     grad_first = grad_second_in + mm(grad_pre, full_in, ((1,), (0,)))
     term_in = mm(grad_pre, first_low, ((0,), (0,))).astype(bf16)
     term_down = mm(hidden_low, grad_ffn, ((0,), (0,))).astype(bf16)
@@ -485,7 +506,7 @@
         term_in,
         term_down,
     ]
-    terms = jnp.concatenate([t.reshape(2, 2, -1, width) for t in parts], axis=2)
+    terms = [t.reshape(2, 2, -1, width) for t in parts]
     vec = jnp.stack(
         [
             jnp.sum(grad_query, axis=0, dtype=f32),

time: 544 us -> 503 us (0.925)
  matrix products: 151 us -> 132 us
  local copies, waits for them, and re-layouts: 55.9 us -> 39 us
  other arithmetic: 35.1 us -> 28.7 us
    dot_general x20, matrix products: 109 us -> 81.2 us  [mm(): return lax.dot_general(a, b, (dims, ((), ())), preferred_element_type=f32)]
    unnamed x95 -> x152, local copies, waits for them, and re-layouts: 29.1 us -> 19.9 us
    concatenate x1 -> x0, local copies, waits for them, and re-layouts: 7.92 us -> none  [local(): terms = jnp.concatenate([t.reshape(2, 2, -1, width) for t in parts], axis=2)]
    dot_general x1, matrix products: 11.1 us -> 16.6 us  [attend_backward(): jnp.einsum('qhd,khd->hqk', grad_heads, split_heads(values), preferred_ele...]
where the time goes in v3:
time: 503 us; the launch traced here: 494 us
  Pallas kernels  292 us (58%)
  matrix products  132 us (26%)
  local copies, waits for them, and re-layouts  39 us (8%)
  other arithmetic  28.7 us (6%)
    pallas_call x1, Pallas kernels, reduce_gradients(): pl.pallas_call(functools.partial(_reduce_kernel, dp_n, slab, heights), ou...  198 us
    pallas_call x1, Pallas kernels, gather_weights(): pl.pallas_call(functools.partial(_gather_kernel, sizes), out_shape=[jax.S...  94 us
    dot_general x20, matrix products, mm(): return lax.dot_general(a, b, (dims, ((), ())), preferred_element_type=f32)  81.2 us
    unnamed x152, local copies, waits for them, and re-layouts  19.9 us
    dot_general x1, matrix products, attend_backward(): jnp.einsum('qhd,khd->hqk', grad_heads, split_heads(values), preferred_ele...  16.6 us
    convert_element_type x1, other arithmetic, attend_backward(): scores_low = grad_scores.astype(jnp.bfloat16)  10.8 us
    slice x2, local copies, waits for them, and re-layouts, local(): shares = [sums[lo:hi] for lo, hi in zip(ends[:-1], ends[1:])]  10.5 us

profile of v3, /device:TPU:0, one launch (start us, length us, event | category | flops | bytes accessed | tf_op | source)
XLA Modules:
  0.0 494.2 jit_solution(15959181386306283198)
XLA Ops:
  0.7 0.7 convert_element_type.237
  1.3 1.3 convert_element_type.235
  2.6 1.6 copy-done
  4.2 1.6 copy-done.1
  5.8 1.0 copy-done.2
  6.9 1.0 copy-done.3
  7.9 1.0 copy-done.4
  9.0 1.0 copy-done.5
  10.0 1.0 copy-done.6
  11.0 94.0 %gather_weights.1 = (bf16[1024,1024]{1,0:T(8,128)(2,1)S(1)}, bf16[1024,1024]{1,0:T(8,128)(2,1)S(1)}, bf16[1024,1024]{1,0:T(8,128)(2,1)S(1)}, bf16[1024,1024]{1,0...) custom-call(bf16[256,1024]{1,0:T(8,128)(2,1)S(1)} %copy-done.2, ...), custom_call_target="tpu_custom_call" | custom-call | tf_op jit(solution)/shard_map/gather_weights/pallas_call | solution.py:110
  105.1 1.3 copy-done.9
  106.4 1.4 copy-done.11
  108.4 0.7 copy-done.7
  109.1 0.6 copy-done.27
  109.8 1.3 add_convert_fusion.1
  111.0 1.3 copy.52
  112.4 3.2 add_convert_fusion
  115.6 1.3 copy.53
  116.9 4.1 convolution_convert_fusion.7
  121.0 1.5 copy.54
  122.6 0.6 dynamic_slice.8
  123.8 8.9 %fusion.42 = (f32[16,512]{1,0:T(8,128)S(1)}, f32[16,512,512]{1,2,0:T(8,128)}) fusion(bf16[512,16,64]{0,2,1:T(8,128)(2,1)} %bitcast.104, bf16[512,16,64]{0,2,1:T(8,128)(2,1)S(1)} %bitcast.100, pred[512]{0:T(512)(128)(4,1)S(1)} %get-tuple-element.90), kind=kOutput, calls=%fused_computation.93 | convolution fusion | flops 549445632 | bytes 18907648 | tf_op jit(solution)/shard_map/qhd,khd->hqk/dot_general | solution.py:354
  132.7 8.4 %fusion = f32[16,512]{1,0:T(8,128)S(1)} fusion(f32[16,512,512]{1,2,0:T(8,128)} %get-tuple-element.73, f32[16,512]{1,0:T(8,128)S(1)} %get-tuple-element.72), kind=kLoop, calls=%fused_computation.6 | loop fusion | flops 8380416 | bytes 16842752 | tf_op jit(solution)/shard_map/reduce_sum | solution.py:364
  141.1 8.1 %fusion.16 = bf16[16,64,512]{2,1,0:T(8,128)(2,1)S(1)} fusion(bf16[512,16,64]{0,2,1:T(8,128)(2,1)S(1)} %bitcast.109, f32[16,512,512]{1,2,0:T(8,128)} %get-tuple-element.73, f32[16,512]{1,0:T(8,128)S(1)} %fusion, f32[16,512]{1,0:T(8,128)S(1)} %get-tuple-element.72), kind=kOutput, calls=%fused_computation.57 | convolution fusion | flops 549978112 | bytes 18939904 | tf_op jit(solution)/shard_map/hqk,khd->qhd/dot_general | solution.py:366
  149.2 1.4 fusion.43
  151.3 10.8 %multiply_convert_fusion.1 = (bf16[512,4096]{1,0:T(8,128)(2,1)S(1)}, f32[512,4096]{1,0:T(8,128)}) fusion(f32[4096]{0:T(1024)S(1)} %copy-done.43, bf16[4096,1024]{1,0:T(8,128)(2,1)} %get-tuple-element.34, f32[512,1024]{1,0:T(8,128)S(1)} %get-tuple-element.75, f32[1024]{0:T(1024)S(1)} %convert_element_type.233, f32[1024]{0:T(1024)S(1)} %convert_element_type.232, ...), kind=kOutput, calls=%fused_computation.18 | convolution fusion | flops 4310171648 | bytes 23097344 | tf_op jit(solution)/shard_map/dot_general | solution.py:438
  162.2 4.8 fusion.44
  167.7 0.6 copy-done.21
  168.3 1.5 multiply_reduce_fusion.1
  169.8 2.0 fusion.36
  171.8 0.8 convert_reduce_fusion.1
  172.7 13.6 %convert_reduce_fusion = (f32[4096]{0:T(1024)}, bf16[512,4096]{1,0:T(8,128)(2,1)}) fusion(f32[512,4096]{1,0:T(8,128)} %get-tuple-element.77, f32[4096]{0:T(1024)S(1)} %copy-done.43, bf16[512,1024]{1,0:T(8,128)(2,1)S(1)} %get-tuple-element.46, bf16[4096,1024]{1,0:T(8,128)(2,1)} %get-tuple-element.35), kind=kOutput, calls=%fused_computation.16 | convolution fusion | flops 4322226176 | bytes 22052864 | tf_op jit(solution)/shard_map/dot_general | solution.py:438
  186.3 7.8 %multiply_reduce_fusion.2 = (f32[1024]{0:T(1024)}, f32[512]{0:T(512)S(1)}, f32[1024]{0:T(1024)}, f32[512,1024]{1,0:T(8,128)S(1)}) fusion(f32[512,1024]{1,0:T(8,128)S(1)} %get-tuple-element.75, f32[512]{0:T(512)S(1)} %fusion.29, f32[512]{0:T(512)S(1)} %broadcast_multiply_fusion.1, f32[1024]{0:T(1024)S(1)} %convert_element_type.232, ...), kind=kOutput, calls=%fused_computation.26 | convolution fusion | flops 4300207616 | bytes 18894848 | tf_op jit(solution)/shard_map/dot_general | solution.py:438
  194.2 0.7 fusion.35
  194.9 1.0 convert_reduce_fusion.2
  196.2 0.7 copy-done.25
  196.9 2.3 convolution_convert_fusion.6
  199.2 1.5 copy.56
  200.7 9.8 %convert_reduce_fusion.3 = (f32[16,64]{1,0:T(8,128)S(1)}, bf16[16,64,512]{2,1,0:T(8,128)(2,1)}) fusion(bf16[512,16,64]{0,2,1:T(8,128)(2,1)S(1)} %bitcast.102, f32[16,512,512]{1,2,0:T(8,128)} %get-tuple-element.73, f32[16,512]{1,0:T(8,128)S(1)} %log_add_fusion), kind=kOutput, calls=%fused_computation.29 | convolution fusion | flops 546831360 | bytes 18911232 | tf_op jit(solution)/shard_map/hqk,qhd->khd/dot_general | solution.py:377
  210.6 16.6 %multiply_reduce_fusion = (f32[16,512]{1,0:T(8,128)}, f32[16,512,512]{1,2,0:T(8,128)}) fusion(f32[16,512,512]{1,2,0:T(8,128)} %get-tuple-element.73, f32[16,512]{1,0:T(8,128)} %copy-done.32, bf16[512,16,64]{0,2,1:T(8,128)(2,1)} %bitcast.103, bf16[512,16,64]{0,2,1:T(8,128)(2,1)} %bitcast.108), kind=kOutput, calls=%fused_computation.1 | convolution fusion | flops 549445632 | bytes 35717120 | tf_op jit(solution)/shard_map/qhd,khd->hqk/dot_general | solution.py:380
  227.1 10.8 %multiply_convert_fusion = bf16[16,512,512]{1,2,0:T(8,128)(2,1)} fusion(f32[16,512,512]{1,2,0:T(8,128)} %get-tuple-element.82, f32[16,512,512]{1,2,0:T(8,128)S(1)} %bitcast.99, f32[16,512]{1,0:T(8,128)} %get-tuple-element.81, f32[16,512]{1,0:T(8,128)} %copy-done.32), kind=kLoop, calls=%fused_computation | loop fusion | flops 16777216 | bytes 42008576 | tf_op jit(solution)/shard_map/convert_element_type | solution.py:384
  238.0 6.2 %multiply_convert_fusion.2 = bf16[16,64,512]{2,1,0:T(8,128)(2,1)S(1)} fusion(bf16[512,16,64]{0,2,1:T(8,128)(2,1)S(1)} %bitcast.105, bf16[16,512,512]{1,2,0:T(8,128)(2,1)} %multiply_convert_fusion), kind=kOutput, calls=%fused_computation.32 | convolution fusion | flops 537919488 | bytes 10485760 | tf_op jit(solution)/shard_map/hqk,qhd->khd/dot_general | solution.py:389
  244.1 1.3 fusion.46
  245.4 2.1 copy-done.13
  247.5 1.5 convert_reduce_fusion.4
  249.1 1.3 fusion.45
  250.7 0.6 copy-done.19
  251.6 2.7 fusion.39
  254.3 2.7 convolution_convert_fusion.5
  257.0 2.7 convolution_convert_fusion.4
  259.7 2.7 convolution_convert_fusion.3
  262.4 2.6 convolution_convert_fusion.2
  265.0 1.0 copy-done.66
  266.0 7.5 %convolution_convert_fusion.1 = bf16[4096,1024]{1,0:T(8,128)(2,1)} fusion(bf16[512,4096]{1,0:T(8,128)(2,1)S(1)} %copy-done.66, f32[512,1024]{1,0:T(8,128)S(1)} %copy-done.15, f32[1024]{0:T(1024)S(1)} %copy-done.54, f32[1024]{0:T(1024)S(1)} %copy-done.46, f32[512]{0:T(512)S(1)} %copy-done.48, f32[512]{0:T(512)S(1)} %copy-done.36), kind=kOutput, calls=%fused_computation.22 | convolution fusion | flops 4301783040 | bytes 14692352 | tf_op jit(solution)/shard_map/dot_general | solution.py:438
  273.6 6.8 %convolution_convert_fusion = bf16[4096,1024]{1,0:T(8,128)(2,1)} fusion(bf16[512,4096]{1,0:T(8,128)(2,1)S(1)} %copy-done.65, bf16[512,1024]{1,0:T(8,128)(2,1)S(1)} %copy-done.24), kind=kOutput, calls=%fused_computation.21 | convolution fusion | flops 4299161600 | bytes 13631488 | tf_op jit(solution)/shard_map/dot_general | solution.py:438
  280.7 0.6 pad.4.refs_6_
  281.4 0.6 reshape.255.refs_7_
  282.0 197.9 %reduce_gradients.1 = (bf16[3072,1024]{1,0:T(8,128)(2,1)}, f32[16,1024]{1,0:T(8,128)}, f32[8,4,1,16,128]{4,3,2,1,0:T(8,128)}) custom-call(bf16[2,2,256,1024]{3,2,1,0:T(8,128)(2,1)} %bitcast.112, bf16[2,2,256,1024]{3,2,1,0:T(8,128)(2,1)} %bitcast.113, bf16[2,2,256,1024]{3,2,1,0:T(8,128)(2,1)} %bitcast.114, bf16[2,2,256,1024]{3,2,1,0:T(8,128)(2,1)} %bitcast.115, ...), custom_call_target="tpu_custom_call" | custom-call | tf_op jit(solution)/shard_map/reduce_gradients/pallas_call | solution.py:311
  479.8 3.8 fusion.38
  483.9 1.3 fusion.26
  485.2 6.7 %fusion.37 = (f32[1024,1024]{1,0:T(8,128)}, f32[1024,1024]{1,0:T(8,128)}) fusion(bf16[3072,1024]{1,0:T(8,128)(2,1)} %get-tuple-element.36), kind=kLoop, calls=%fused_computation.88 | loop fusion | bytes 16777216 | tf_op jit(solution)/shard_map/slice | solution.py:536
  491.9 0.6 fusion.41
  492.5 0.6 convert_reduce_fusion.5
  493.2 0.6 copy.77
  (169 shorter events, 3.7 us)
Async XLA Ops:
  2.6 1.6 copy-start
  4.2 1.6 copy-start.1
  11.0 96.7 %copy-start.55 = (bf16[1024]{0:T(1024)(128)(2,1)S(1)}, bf16[1024]{0:T(1024)(128)(2,1)}, u32[]{:S(2)}) copy-start(bf16[1024]{0:T(1024)(128)(2,1)} %param.34) | copy-start | bytes 6148
  11.0 96.7 %copy-start.56 = (bf16[1024]{0:T(1024)(128)(2,1)S(1)}, bf16[1024]{0:T(1024)(128)(2,1)}, u32[]{:S(2)}) copy-start(bf16[1024]{0:T(1024)(128)(2,1)} %param.33) | copy-start | bytes 6148
  11.0 96.8 %copy-start.41 = (bf16[1,1024]{1,0:T(2,128)(2,1)S(1)}, bf16[1,1024]{1,0:T(2,128)(2,1)}, u32[]{:S(2)}) copy-start(bf16[1,1024]{1,0:T(2,128)(2,1)} %param.22) | copy-start | bytes 6148
  105.1 1.4 copy-start.9
  106.4 1.4 copy-start.11
  107.8 1.4 copy-start.7
  107.8 2.0 copy-start.27
  111.0 1.3 copy-start.58
  121.0 1.5 copy-start.63
  132.7 8.4 %copy-start.20 = (bf16[512,1024]{0,1:T(8,128)(2,1)S(1)}, bf16[512,1024]{0,1:T(8,128)(2,1)}, u32[]{:S(2)}) copy-start(bf16[512,1024]{0,1:T(8,128)(2,1)} %copy.52) | copy-start | bytes 3145732
  141.1 8.1 %copy-start.28 = (bf16[512,1024]{1,0:T(8,128)(2,1)S(1)}, bf16[512,1024]{1,0:T(8,128)(2,1)}, u32[]{:S(2)}) copy-start(bf16[512,1024]{1,0:T(8,128)(2,1)} %param.21) | copy-start | bytes 3145732
  149.1 1.4 copy-start.30
  149.2 1.5 copy-start.59
  149.2 1.5 copy-start.60
  150.6 43.6 %copy-start.14 = (f32[512,1024]{1,0:T(8,128)}, f32[512,1024]{1,0:T(8,128)S(1)}, u32[]{:S(2)}) copy-start(f32[512,1024]{1,0:T(8,128)S(1)} %get-tuple-element.75) | copy-start | bytes 6291460
  150.6 11.5 %copy-start.53 = (f32[1024]{0:T(1024)}, f32[1024]{0:T(1024)S(1)}, u32[]{:S(2)}) copy-start(f32[1024]{0:T(1024)S(1)} %convert_element_type.233) | copy-start | bytes 12292
  150.7 43.5 %copy-start.45 = (f32[1024]{0:T(1024)}, f32[1024]{0:T(1024)S(1)}, u32[]{:S(2)}) copy-start(f32[1024]{0:T(1024)S(1)} %convert_element_type.232) | copy-start | bytes 12292
  150.7 43.5 %copy-start.35 = (f32[512]{0:T(512)}, f32[512]{0:T(512)S(1)}, u32[]{:S(2)}) copy-start(f32[512]{0:T(512)S(1)} %broadcast_multiply_fusion.1) | copy-start | bytes 6148
  150.7 11.5 %slice-start.6 = ((s8[8388608]{0:T(1024)(128)(4,1)}), s8[4194304]{0:T(1024)(128)(4,1)S(1)}, s32[]{:S(2)}) async-start(s8[8388608]{0:T(1024)(128)(4,1)} %bitcast.141), calls=%async_computation.6 | async-start | bytes 8388608
  151.3 42.8 %copy-start.47 = (f32[512]{0:T(512)}, f32[512]{0:T(512)S(1)}, u32[]{:S(2)}) copy-start(f32[512]{0:T(512)S(1)} %fusion.29) | copy-start | bytes 6148
  151.3 10.8 %slice-start.7 = ((s8[8388608]{0:T(1024)(128)(4,1)}), s8[4194304]{0:T(1024)(128)(4,1)S(1)}, s32[]{:S(2)}) async-start(s8[8388608]{0:T(1024)(128)(4,1)} %bitcast.141), calls=%async_computation.7 | async-start | bytes 8388608
  162.2 4.8 copy-start.64
  167.4 2.4 copy-start.62
  171.8 14.5 %slice-start.4 = ((s8[8388608]{0:T(1024)(128)(4,1)}), s8[4194304]{0:T(1024)(128)(4,1)S(1)}, s32[]{:S(2)}) async-start(s8[8388608]{0:T(1024)(128)(4,1)} %bitcast.139), calls=%async_computation.4 | async-start | bytes 8388608
  172.6 13.7 %copy-start.23 = (bf16[512,1024]{1,0:T(8,128)(2,1)}, bf16[512,1024]{1,0:T(8,128)(2,1)S(1)}, u32[]{:S(2)}) copy-start(bf16[512,1024]{1,0:T(8,128)(2,1)S(1)} %get-tuple-element.46) | copy-start | bytes 3145732
  172.6 13.7 %slice-start.5 = ((s8[8388608]{0:T(1024)(128)(4,1)}), s8[4194304]{0:T(1024)(128)(4,1)S(1)}, s32[]{:S(2)}) async-start(s8[8388608]{0:T(1024)(128)(4,1)} %bitcast.139), calls=%async_computation.5 | async-start | bytes 8388608
  194.9 4.3 copy-start.49
  200.7 9.9 %copy-start.16 = (bf16[512,1024]{0,1:T(8,128)(2,1)}, bf16[512,1024]{0,1:T(8,128)(2,1)S(1)}, u32[]{:S(2)}) copy-start(bf16[512,1024]{0,1:T(8,128)(2,1)S(1)} %copy.56) | copy-start | bytes 3145732
  200.7 9.8 %copy-start.32 = (f32[16,512]{1,0:T(8,128)}, f32[16,512]{1,0:T(8,128)S(1)}, u32[]{:S(2)}) copy-start(f32[16,512]{1,0:T(8,128)S(1)} %log_add_fusion) | copy-start | bytes 98308
  210.5 16.6 %slice-start = ((s8[16777216]{0:T(1024)(128)(4,1)}), s8[4194304]{0:T(1024)(128)(4,1)S(1)}, s32[]{:S(2)}) async-start(s8[16777216]{0:T(1024)(128)(4,1)} %bitcast.98), calls=%async_computation | async-start | bytes 8388608
  210.5 16.6 %slice-start.1 = ((s8[16777216]{0:T(1024)(128)(4,1)}), s8[4194304]{0:T(1024)(128)(4,1)S(1)}, s32[]{:S(2)}) async-start(s8[16777216]{0:T(1024)(128)(4,1)} %bitcast.98), calls=%async_computation.1 | async-start | bytes 8388608
  210.5 16.6 %slice-start.2 = ((s8[16777216]{0:T(1024)(128)(4,1)}), s8[4194304]{0:T(1024)(128)(4,1)S(1)}, s32[]{:S(2)}) async-start(s8[16777216]{0:T(1024)(128)(4,1)} %bitcast.98), calls=%async_computation.2 | async-start | bytes 8388608
  210.5 16.6 %slice-start.3 = ((s8[16777216]{0:T(1024)(128)(4,1)}), s8[4194304]{0:T(1024)(128)(4,1)S(1)}, s32[]{:S(2)}) async-start(s8[16777216]{0:T(1024)(128)(4,1)} %bitcast.98), calls=%async_computation.3 | async-start | bytes 8388608
  227.1 10.8 %copy-start.17 = (bf16[512,1024]{0,1:T(8,128)(2,1)S(1)}, bf16[512,1024]{0,1:T(8,128)(2,1)}, u32[]{:S(2)}) copy-start(bf16[512,1024]{0,1:T(8,128)(2,1)} %copy.53) | copy-start | bytes 3145732
  238.0 6.2 %copy-start.12 = (bf16[1024,1024]{1,0:T(8,128)(2,1)S(1)}, bf16[1024,1024]{1,0:T(8,128)(2,1)}, u32[]{:S(2)}) copy-start(bf16[1024,1024]{1,0:T(8,128)(2,1)} %copy-done.11) | copy-start | bytes 6291460
  244.1 3.4 copy-start.13
  247.5 1.6 copy-start.10
  249.1 1.6 copy-start.8
  249.1 2.2 copy-start.19
  249.1 2.5 copy-start.22
  249.1 2.5 copy-start.50
  251.6 2.7 copy-start.29
  259.7 2.7 copy-start.26
  259.7 2.7 copy-start.31
  262.4 2.6 copy-start.15
  262.4 2.6 copy-start.36
  262.4 2.6 copy-start.46
  262.4 2.6 copy-start.48
  262.4 2.6 copy-start.54
  262.4 3.6 copy-start.66
  266.0 7.5 %copy-start.24 = (bf16[512,1024]{1,0:T(8,128)(2,1)S(1)}, bf16[512,1024]{1,0:T(8,128)(2,1)}, u32[]{:S(2)}) copy-start(bf16[512,1024]{1,0:T(8,128)(2,1)} %copy-done.23) | copy-start | bytes 3145732
  266.0 7.5 %copy-start.65 = (bf16[512,4096]{1,0:T(8,128)(2,1)S(1)}, bf16[512,4096]{1,0:T(8,128)(2,1)}, u32[]{:S(2)}) copy-start(bf16[512,4096]{1,0:T(8,128)(2,1)} %copy-done.64) | copy-start | bytes 12582916
  273.5 7.0 %copy-start.44 = (f32[4096]{0:T(1024)S(1)}, f32[4096]{0:T(1024)}, u32[]{:S(2)}) copy-start(f32[4096]{0:T(1024)} %get-tuple-element.88) | copy-start | bytes 49156
  273.5 7.0 %copy-start.37 = (f32[1024]{0:T(1024)S(1)}, f32[1024]{0:T(1024)}, u32[]{:S(2)}) copy-start(f32[1024]{0:T(1024)} %get-tuple-element.41) | copy-start | bytes 12292
  273.5 7.0 %copy-start.38 = (f32[1024]{0:T(1024)S(1)}, f32[1024]{0:T(1024)}, u32[]{:S(2)}) copy-start(f32[1024]{0:T(1024)} %get-tuple-element.44) | copy-start | bytes 12292
  273.6 7.0 %copy-start.39 = (f32[1024]{0:T(1024)S(1)}, f32[1024]{0:T(1024)}, u32[]{:S(2)}) copy-start(f32[1024]{0:T(1024)} %get-tuple-element.45) | copy-start | bytes 12292
  273.6 7.0 %copy-start.40 = (f32[1024]{0:T(1024)S(1)}, f32[1024]{0:T(1024)}, u32[]{:S(2)}) copy-start(f32[1024]{0:T(1024)} %get-tuple-element.47) | copy-start | bytes 12292
  273.6 7.0 %copy-start.51 = (f32[1024]{0:T(1024)S(1)}, f32[1024]{0:T(1024)}, u32[]{:S(2)}) copy-start(f32[1024]{0:T(1024)} %get-tuple-element.39) | copy-start | bytes 12292
  273.6 7.0 %copy-start.52 = (f32[1024]{0:T(1024)S(1)}, f32[1024]{0:T(1024)}, u32[]{:S(2)}) copy-start(f32[1024]{0:T(1024)} %get-tuple-element.43) | copy-start | bytes 12292
  273.6 7.7 %copy-start.42 = (bf16[1,1024]{1,0:T(2,128)(2,1)S(1)}, bf16[1,1024]{1,0:T(2,128)(2,1)}, u32[]{:S(2)}) copy-start(bf16[1,1024]{1,0:T(2,128)(2,1)} %param.22) | copy-start | bytes 6148
  479.8 3.8 copy-start.33
  485.2 6.7 %copy-start.34 = (f32[16,1024]{1,0:T(8,128)S(1)}, f32[16,1024]{1,0:T(8,128)}, u32[]{:S(2)}) copy-start(f32[16,1024]{1,0:T(8,128)} %get-tuple-element.38) | copy-start | bytes 196612
  (11 other events, 10.8 us)
